TPU v7x, 128 devices: a whole 4x4x4 slice. The times are simulated.
128 devices in a mesh: seq: 16 (over y, z), batch: 8 (over x, core).
Axes of the slice: x: 4, y: 4, z: 4, core: 2. Of those that a mesh axis runs over, the one named last changes fastest.
Arguments:
- inputs: bfloat16 [8, 16384, 2048], P('batch', 'seq'), may hold values from -6 to 6
- input_map: bfloat16 [8, 16384, 128], P('batch', 'seq'), may hold values from -0.5 to 0.5
- output_map: bfloat16 [8, 16384, 128], P('batch', 'seq'), may hold values from -0.5 to 0.5
- step_raw: float32 [8, 32, 16384], P('batch', None, 'seq'), may hold values from -4.5 to 4.5
- step_bias: float32 [32], replicated, may hold values from -2 to 0
- decay_rate: float32 [32], replicated, may hold values from 1.5258789e-05 to 0.05
- skip_gain: float32 [32], replicated, may hold values from 0.5 to 1.5
- cotangent: bfloat16 [8, 16384, 2048], P('batch', 'seq'), may hold values from -6 to 6
Outputs:
- grad_inputs: bfloat16 [8, 16384, 2048], P('batch', 'seq')
- grad_input_map: float32 [8, 16384, 128], P('batch', 'seq')
- grad_output_map: float32 [8, 16384, 128], P('batch', 'seq')
- grad_step_raw: float32 [8, 32, 16384], P('batch', None, 'seq')
- grad_params: float32 [2, 32], replicated
- grad_decay_rate: float32 [32], replicated
All inputs are finite; a program needn't handle non-finite values.
Results may differ from a plain program's by a relative error of at most 0.034.
Values sent between devices are 32-bit elements; how exact they have to be, the bound alone decides.
A program may use at most 192 MiB of HBM per device.

v0:
```python
import math

import jax
import jax.numpy as jnp
from jax import lax
from jax.sharding import PartitionSpec as P

GROUP = 256


def entering(array, axis, combine, identity, reverse):
    length, mine = (lax.axis_size(axis), lax.axis_index(axis))
    everything = jax.tree.map(lambda part: lax.all_gather(part, axis), array)
    start = jax.tree.map(
        lambda part, zero: jnp.broadcast_to(jnp.asarray(zero, part.dtype), part.shape),
        array,
        identity,
    )

    def lap(k, before):
        at = length - 1 - k if reverse else k
        reached = at > mine if reverse else at < mine
        new = combine(before, jax.tree.map(lambda part: part[at], everything))
        return jax.tree.map(lambda a, b: jnp.where(reached, a, b), new, before)

    return lax.fori_loop(0, length, lap, start)


def block_step(state, items, skip_gain):
    xc, bc, cc, stepc, logc = items
    width = xc.shape[0]
    cum = jnp.cumsum(logc, axis=1)
    rows = lax.broadcasted_iota(jnp.int32, (width, width), 0)
    cols = lax.broadcasted_iota(jnp.int32, (width, width), 1)
    lower = cols <= rows
    gap = jnp.where(lower[None], cum[:, :, None] - cum[:, None, :], -1e30)
    decay = jnp.exp(gap)
    scores = jnp.einsum("tn,sn->ts", cc, bc, preferred_element_type=jnp.float32)
    weights = (scores[None] * decay * stepc[:, None, :]).astype(jnp.bfloat16)
    inner = jnp.einsum("hts,shp->thp", weights, xc, preferred_element_type=jnp.float32)
    carried = (
        jnp.einsum(
            "tn,hpn->thp", cc, state.astype(jnp.bfloat16), preferred_element_type=jnp.float32
        )
        * jnp.exp(cum).T[:, :, None]
    )
    output = inner + carried + skip_gain[None, :, None] * xc.astype(jnp.float32)
    tail = jnp.exp(cum[:, -1:] - cum) * stepc
    scaled = (xc.astype(jnp.float32) * tail.T[:, :, None]).astype(jnp.bfloat16)
    fresh = jnp.einsum("shp,sn->hpn", scaled, bc, preferred_element_type=jnp.float32)
    new_state = jnp.exp(cum[:, -1])[:, None, None] * state + fresh
    return (new_state, output.astype(jnp.bfloat16))


def scan_forward(xb, bb, cb, raw, step_bias, decay_rate, skip_gain, start_state):
    length, heads, head_size = xb.shape
    states = bb.shape[1]
    blocks = length // GROUP
    step = jax.nn.softplus(raw + step_bias[:, None])
    logd = -decay_rate[:, None] * step
    xs = xb.reshape(blocks, GROUP, heads, head_size)
    bs = bb.reshape(blocks, GROUP, states)
    cs = cb.reshape(blocks, GROUP, states)
    steps = step.reshape(heads, blocks, GROUP).transpose(1, 0, 2)
    logs = logd.reshape(heads, blocks, GROUP).transpose(1, 0, 2)
    body_fn = jax.checkpoint(lambda s, it: block_step(s, it, skip_gain))
    end_state, outs = lax.scan(body_fn, start_state, (xs, bs, cs, steps, logs))
    return (outs.reshape(length, heads, head_size), end_state)


def carry_combine(earlier, later):
    total_e, state_e = earlier
    total_l, state_l = later
    return (total_e + total_l, jnp.exp(total_l)[:, None, None] * state_e + state_l)


def shards(inputs, input_map, output_map, step_raw, step_bias, decay_rate, skip_gain, cotangent):
    length = inputs.shape[1]
    width = inputs.shape[2]
    heads = step_raw.shape[1]
    head_size = width // heads
    states = input_map.shape[2]
    xb = inputs[0].reshape(length, heads, head_size)
    bb = input_map[0]
    cb = output_map[0]
    dyb = cotangent[0].reshape(length, heads, head_size)
    raw = step_raw[0]
    step = jax.nn.softplus(raw + step_bias[:, None])
    logd = -decay_rate[:, None] * step
    cum = jnp.cumsum(logd, axis=1)
    total = cum[:, -1]
    weight_in = jnp.exp(total[:, None] - cum) * step
    scaled_in = (xb.astype(jnp.float32) * weight_in.T[:, :, None]).astype(jnp.bfloat16)
    local_state = jnp.einsum("shp,sn->hpn", scaled_in, bb, preferred_element_type=jnp.float32)
    scaled_grad = dyb.astype(jnp.float32) * jnp.exp(cum).T[:, :, None]
    local_grad = jnp.einsum("thp,tn->hpn", scaled_grad, cb, preferred_element_type=jnp.float32)
    zero_state = jnp.zeros((heads, head_size, states), jnp.float32)
    zero_total = jnp.zeros((heads,), jnp.float32)
    start_state = entering(
        (total, local_state), "seq", carry_combine, (zero_total, zero_state), False
    )[1]
    end_grad = entering((total, local_grad), "seq", carry_combine, (zero_total, zero_state), True)[
        1
    ]

    def local_forward(xv, bv, cv, rv, biasv, ratev, skipv):
        return scan_forward(xv, bv, cv, rv, biasv, ratev, skipv, start_state)

    outputs, pull = jax.vjp(local_forward, xb, bb, cb, raw, step_bias, decay_rate, skip_gain)
    grads = pull((dyb, end_grad))
    params = jnp.stack([grads[4], grads[5], grads[6]])
    total_tokens = length * lax.axis_size("seq") * lax.axis_size("batch")
    summed = lax.psum(params, ("seq", "batch")) * (1.0 / math.sqrt(total_tokens))
    grad_inputs = grads[0].reshape(length, width)[None]
    pair = jnp.stack([summed[0], summed[2]])
    return (
        grad_inputs,
        grads[1].astype(jnp.float32)[None],
        grads[2].astype(jnp.float32)[None],
        grads[3][None],
        pair,
        summed[1],
    )


def solution(mesh):
    in_specs = (
        P("batch", "seq", None),
        P("batch", "seq", None),
        P("batch", "seq", None),
        P("batch", None, "seq"),
        P(),
        P(),
        P(),
        P("batch", "seq", None),
    )
    out_specs = (
        P("batch", "seq", None),
        P("batch", "seq", None),
        P("batch", "seq", None),
        P("batch", None, "seq"),
        P(),
        P(),
    )
    return jax.shard_map(shards, mesh=mesh, in_specs=in_specs, out_specs=out_specs, check_vma=False)
```

profile of v0, /device:TPU:1, one launch (start us, length us, event | category | flops | bytes accessed | tf_op | source)
XLA Modules:
  0.0 635.8 jit_solution(4650788162293645006)
XLA Ops:
  9.6 9.0 %reduce-window.64 = f32[32,8,128]{2,1,0:T(8,128)S(1)} reduce-window(f32[32,8,128]{2,1,0:T(8,128)S(1)} %fusion.79, f32[]{:T(128)} %constant.177.clone.1), window={size=1x1x128 pad=0_0x0_0x127_0}, to_apply=%region_0.1 | reduce-window | flops 4161536 | bytes 262148 | tf_op jit(solution)/shard_map/reduce-window.6
  20.4 6.4 %copy.157 = bf16[1,1024,2048]{1,2,0:T(8,128)(2,1)} copy(bf16[1,1024,2048]{2,1,0:T(8,128)(2,1)} %param.16) | data formatting | bytes 8388608 | tf_op args[0]
  26.8 3.4 fusion.74
  30.2 3.2 fusion.75
  33.4 6.4 %copy.156 = bf16[1,1024,2048]{1,2,0:T(8,128)(2,1)} copy(bf16[1,1024,2048]{2,1,0:T(8,128)(2,1)} %param.23) | data formatting | bytes 8388608 | tf_op args[7]
  39.9 3.4 bitcast_multiply_fusion.5
  43.2 3.2 fusion.77
  46.6 8.0 %reshape_reshape_squeeze.6 = bf16[4,256,32,64]{1,0,3,2:T(4,128)(2,1)} reshape(bf16[1,1024,2048]{1,2,0:T(8,128)(2,1)} %copy.157) | data formatting | bytes 8388608 | tf_op jit(solution)/shard_map/jvp()/reshape;reshape;squeeze | solution.py:61
  54.6 12.9 %reshape.416 = bf16[4,256,32,64]{3,2,1,0:T(8,128)(2,1)} reshape(bf16[1,1024,2048]{2,1,0:T(8,128)(2,1)} %param.23) | data formatting | bytes 8388608 | tf_op jit(solution)/shard_map/transpose(jvp())/reshape;reshape;squeeze | solution.py:68
  69.0 36.4 %all-reduce.2 = f32[512]{0:T(512)S(1)} all-reduce(f32[512]{0:T(512)S(1)} %dynamic-update-slice), channel_id=2, replica_groups=mesh['seq'=16,'batch'=8] {'seq'}, use_global_device_ids=true, to_apply=%add.2 | all-reduce | flops 512 | bytes 4096
  107.1 4.9 copy.160
  112.0 10.4 %copy.167 = bf16[4,256,32,64]{1,3,2,0:T(8,128)(2,1)} copy(bf16[4,256,32,64]{3,2,1,0:T(8,128)(2,1)} %reshape.416) | data formatting | bytes 8388608
  122.4 26.4 %all-gather.8.cloned.1.call-done = f32[512,64,128]{2,1,0:T(8,128)} async-done(((f32[32,64,128]{2,1,0:T(8,128)}), f32[512,64,128]{2,1,0:T(8,128)}) %all-gather.8.cloned.1.call-update) | async-done | bytes 16777232 | tf_op jit(solution)/shard_map/all_gather | solution.py:13
  148.8 24.5 %while.71 = (s32[]{:T(128)}, f32[32,64,128]{2,1,0:T(8,128)S(1)}, s32[]{:T(128)}, f32[16,32]{1,0:T(8,128)S(1)}, f32[16,32,64,128]{3,2,1,0:T(8,128)}, /*index=5*/s32[]{:T(128)}, s32[]{:T(128)}) while((s32[]{:T(128)}, f32[32,64,128]{2,1,0:T(8,128)S(1)}, s32[]{:T(128)}, f32[16,32]{1,0:T(8,128)S(1)}, f32[16,32,64,128]{3,2,1,0:T(8,128)}, ...), condition=%wide.region_5.6_spmd.clone, body=%wide.region_4.5_spmd.clone.sunk | while | flops 1048580 | bytes 3146225 | solution.py:26
  173.3 88.7 %all-gather.6.cloned.1.call-done = f32[512,64,128]{2,1,0:T(8,128)} async-done(((f32[32,64,128]{2,1,0:T(8,128)}), f32[512,64,128]{2,1,0:T(8,128)}) %all-gather.6.cloned.1.call-update) | async-done | bytes 16777232 | tf_op jit(solution)/shard_map/all_gather | solution.py:13
  261.9 24.2 %while.70 = (s32[]{:T(128)}, f32[32,64,128]{2,1,0:T(8,128)S(1)}, s32[]{:T(128)}, f32[16,32]{1,0:T(8,128)S(1)}, f32[16,32,64,128]{3,2,1,0:T(8,128)}, /*index=5*/s32[]{:T(128)}, s32[]{:T(128)}, s32[]{:T(128)}, s32[]{:T(128)}) while((s32[]{:T(128)}, f32[32,64,128]{2,1,0:T(8,128)S(1)}, s32[]{:T(128)}, f32[16,32]{1,0:T(8,128)S(1)}, ...), condition=%wide.region_3.4_spmd.clone, body=%wide.region_2.3_spmd.clone.sunk | while | flops 1048584 | bytes 3146287 | solution.py:26
  286.2 23.5 %while.69 = (s32[]{:T(128)}, f32[32,64,128]{2,1,0:T(8,128)S(1)}, f32[4,32,64,128]{3,2,1,0:T(8,128)}, f32[4,32,256]{2,1,0:T(8,128)}, bf16[4,256,32,64]{1,3,2,0:T(...) while((s32[]{:T(128)}, f32[32,64,128]{2,1,0:T(8,128)S(1)}, ...), condition=%wide.region_9.10_spmd, body=%wide.region_6.9_spmd.sunk | while | flops 137388128 | bytes 5836793 | solution.py:67
  312.5 2.5 broadcast_in_dim.122
  315.0 217.0 %while.72 = (s32[]{:T(128)}, f32[32]{0:T(128)S(1)}, f32[32,64,128]{2,1,0:T(8,128)S(1)}, bf16[4,256,32,64]{1,3,2,0:T(8,128)(2,1)}, bf16[4,256,128]{2,1,0:T(8,128)...) while((s32[]{:T(128)}, f32[32]{0:T(128)S(1)}, ...), condition=%wide.region_24.25_spmd.clone, body=%wide.region_10.0_spmd.clone.sunk | while | flops 1320558848 | bytes 38805324 | solution.py:67
  319.6 2.7 dynamic-slice_bitcast_fusion.11
  327.6 8.2 %fusion.164 = (f32[32,256]{1,0:T(8,128)}, f32[32,256]{1,0:T(8,128)}, f32[32,256]{1,0:T(8,128)}, bf16[256,256]{1,0:T(8,128)(2,1)S(1)}) fusion(f32[32,256]{1,0:T(8,128)} %copy.233, f32[32,256]{1,0:T(8,128)} %copy_bitcast_fusion.10, f32[256,256]{1,0:T(8,128)S(1)} %fusion.163, pred[256,256]{1,0:T(8,128)(4,1)} %iota_compare_fusion.2, ...), kind=kOutput, calls=%fused_computation.36.clone.1 | convolution fusion | flops 299802624 | bytes 2719744 | tf_op jit(solution)/shard_map/transpose(jvp())/while/body/eval_jaxpr/checkpoint/hts,shp->thp/dot_general | solution.py:40
  341.9 3.6 fusion.161
  348.0 2.0 fusion.167
  354.7 2.4 fusion.172
  357.8 2.5 reduce-window.80
  364.6 4.6 fusion.170
  373.9 2.7 dynamic-slice_bitcast_fusion.11
  381.9 8.2 %fusion.164 = (f32[32,256]{1,0:T(8,128)}, f32[32,256]{1,0:T(8,128)}, f32[32,256]{1,0:T(8,128)}, bf16[256,256]{1,0:T(8,128)(2,1)S(1)}) fusion(f32[32,256]{1,0:T(8,128)} %copy.233, f32[32,256]{1,0:T(8,128)} %copy_bitcast_fusion.10, f32[256,256]{1,0:T(8,128)S(1)} %fusion.163, pred[256,256]{1,0:T(8,128)(4,1)} %iota_compare_fusion.2, ...), kind=kOutput, calls=%fused_computation.36.clone.1 | convolution fusion | flops 299802624 | bytes 2719744 | tf_op jit(solution)/shard_map/transpose(jvp())/while/body/eval_jaxpr/checkpoint/hts,shp->thp/dot_general | solution.py:40
  396.2 3.6 fusion.161
  402.2 2.0 fusion.167
  408.9 2.4 fusion.172
  412.0 2.5 reduce-window.80
  418.8 4.6 fusion.170
  428.1 2.7 dynamic-slice_bitcast_fusion.11
  436.1 8.2 %fusion.164 = (f32[32,256]{1,0:T(8,128)}, f32[32,256]{1,0:T(8,128)}, f32[32,256]{1,0:T(8,128)}, bf16[256,256]{1,0:T(8,128)(2,1)S(1)}) fusion(f32[32,256]{1,0:T(8,128)} %copy.233, f32[32,256]{1,0:T(8,128)} %copy_bitcast_fusion.10, f32[256,256]{1,0:T(8,128)S(1)} %fusion.163, pred[256,256]{1,0:T(8,128)(4,1)} %iota_compare_fusion.2, ...), kind=kOutput, calls=%fused_computation.36.clone.1 | convolution fusion | flops 299802624 | bytes 2719744 | tf_op jit(solution)/shard_map/transpose(jvp())/while/body/eval_jaxpr/checkpoint/hts,shp->thp/dot_general | solution.py:40
  450.4 3.6 fusion.161
  463.2 2.4 fusion.172
  466.3 2.5 reduce-window.80
  473.1 4.6 fusion.170
  482.4 2.7 dynamic-slice_bitcast_fusion.11
  490.4 8.2 %fusion.164 = (f32[32,256]{1,0:T(8,128)}, f32[32,256]{1,0:T(8,128)}, f32[32,256]{1,0:T(8,128)}, bf16[256,256]{1,0:T(8,128)(2,1)S(1)}) fusion(f32[32,256]{1,0:T(8,128)} %copy.233, f32[32,256]{1,0:T(8,128)} %copy_bitcast_fusion.10, f32[256,256]{1,0:T(8,128)S(1)} %fusion.163, pred[256,256]{1,0:T(8,128)(4,1)} %iota_compare_fusion.2, ...), kind=kOutput, calls=%fused_computation.36.clone.1 | convolution fusion | flops 299802624 | bytes 2719744 | tf_op jit(solution)/shard_map/transpose(jvp())/while/body/eval_jaxpr/checkpoint/hts,shp->thp/dot_general | solution.py:40
  504.7 3.6 fusion.161
  517.4 2.4 fusion.172
  520.5 2.5 reduce-window.80
  527.3 4.6 fusion.170
  533.9 64.8 %psum.7 = f32[3,32]{1,0:T(4,128)S(1)} all-reduce(f32[3,32]{1,0:T(4,128)S(1)} %pad_maximum_fusion), channel_id=1, replica_groups=mesh['seq'=16,'batch'=8] {'seq','batch'}, use_global_device_ids=true, to_apply=%region_27.28 | all-reduce | flops 96 | bytes 768 | tf_op jit(solution)/shard_map/psum | solution.py:113
  601.2 12.9 %copy.174 = bf16[4,256,32,64]{3,2,1,0:T(8,128)(2,1)} copy(bf16[4,256,32,64]{1,3,2,0:T(8,128)(2,1)} %get-tuple-element.598) | data formatting | bytes 8388608
  614.1 12.4 %reshape.417 = bf16[1,1024,2048]{2,1,0:T(8,128)(2,1)} reshape(bf16[4,256,32,64]{3,2,1,0:T(8,128)(2,1)} %copy.174) | data formatting | bytes 8388608
  (403 shorter events, 203.9 us)
Async XLA Ops:
  7.2 141.7 %all-gather.8.cloned.1.call-start = ((), (), s32[]{:S(2)}) async-start(), calls=%async_computation.1 | async-start | bytes 17825792 | tf_op jit(solution)/shard_map/all_gather | solution.py:13
  7.9 97.6 %copy-start.13 = (f32[32]{0:T(128)}, f32[32]{0:T(128)S(1)}, u32[]{:S(2)}) copy-start(f32[32]{0:T(128)S(1)} %neg.50) | copy-start | bytes 388
  33.4 228.6 %all-gather.6.cloned.1.call-start = ((), (), s32[]{:S(2)}) async-start(), calls=%async_computation | async-start | bytes 17825792 | tf_op jit(solution)/shard_map/all_gather | solution.py:13
  43.2 3.3 copy-start.5
  46.6 58.9 %copy-start.7 = (f32[32,4,256]{2,1,0:T(4,128)}, f32[32,4,256]{2,1,0:T(4,128)S(1)}, u32[]{:S(2)}) copy-start(f32[32,4,256]{2,1,0:T(4,128)S(1)} %squeeze.124) | copy-start | bytes 393220
  54.6 12.9 %copy-start.16 = (u32[128]{0:T(128)S(1)}, u32[128]{0:T(128)}, u32[]{:S(2)}) copy-start(u32[128]{0:T(128)} %constant.194) | copy-start | bytes 1540
  54.6 50.9 %copy-start.10 = (f32[32]{0:T(128)S(1)}, f32[32]{0:T(128)}, u32[]{:S(2)}) copy-start(f32[32]{0:T(128)} %param.20) | copy-start | bytes 388
  327.6 8.2 %copy-start.3 = (f32[256,256]{1,0:T(8,128)}, f32[256,256]{1,0:T(8,128)S(1)}, u32[]{:S(2)}) copy-start(f32[256,256]{1,0:T(8,128)S(1)} %fusion.163) | copy-start | bytes 786436 | tf_op jit(solution)/shard_map/transpose(jvp())/while
  345.5 18.4 %copy-start.12 = (f32[32]{0:T(128)S(1)}, f32[32]{0:T(128)}, u32[]{:S(2)}) copy-start(f32[32]{0:T(128)} %fusion.168) | copy-start | bytes 388 | tf_op jit(solution)/shard_map/transpose(jvp())/while
  350.0 7.1 %copy-start.2 = (f32[1,32,256]{1,2,0:T(8,128)S(1)}, f32[1,32,256]{1,2,0:T(8,128)}, u32[]{:S(2)}) copy-start(f32[1,32,256]{1,2,0:T(8,128)} %get-tuple-element.1214) | copy-start | bytes 98308 | tf_op jit(solution)/shard_map/transpose(jvp())/while
  350.0 7.7 %copy-start.1 = (f32[32,256]{0,1:T(8,128)S(1)}, f32[32,256]{0,1:T(8,128)}, u32[]{:S(2)}) copy-start(f32[32,256]{0,1:T(8,128)} %get-tuple-element.1215) | copy-start | bytes 98308 | tf_op jit(solution)/shard_map/transpose(jvp())/while
  351.0 13.6 %copy-start.4 = (f32[32,256]{1,0:T(8,128)S(1)}, f32[32,256]{1,0:T(8,128)}, u32[]{:S(2)}) copy-start(f32[32,256]{1,0:T(8,128)} %copy_bitcast_fusion.10) | copy-start | bytes 98308 | tf_op jit(solution)/shard_map/transpose(jvp())/while
  351.0 13.6 %copy-start.15 = (f32[32]{0:T(128)S(1)}, f32[32]{0:T(128)}, u32[]{:S(2)}) copy-start(f32[32]{0:T(128)} %get-tuple-element.1211) | copy-start | bytes 388 | tf_op jit(solution)/shard_map/transpose(jvp())/while
  353.0 11.6 %copy-start = (bf16[256,32,64]{0,2,1:T(8,128)(2,1)S(1)}, bf16[256,32,64]{0,2,1:T(8,128)(2,1)}, u32[]{:S(2)}) copy-start(bf16[256,32,64]{0,2,1:T(8,128)(2,1)} %get-tuple-element.1210) | copy-start | bytes 3145732 | tf_op jit(solution)/shard_map/transpose(jvp())/while
  381.9 8.2 %copy-start.3 = (f32[256,256]{1,0:T(8,128)}, f32[256,256]{1,0:T(8,128)S(1)}, u32[]{:S(2)}) copy-start(f32[256,256]{1,0:T(8,128)S(1)} %fusion.163) | copy-start | bytes 786436 | tf_op jit(solution)/shard_map/transpose(jvp())/while
  399.8 18.4 %copy-start.12 = (f32[32]{0:T(128)S(1)}, f32[32]{0:T(128)}, u32[]{:S(2)}) copy-start(f32[32]{0:T(128)} %fusion.168) | copy-start | bytes 388 | tf_op jit(solution)/shard_map/transpose(jvp())/while
  404.2 7.1 %copy-start.2 = (f32[1,32,256]{1,2,0:T(8,128)S(1)}, f32[1,32,256]{1,2,0:T(8,128)}, u32[]{:S(2)}) copy-start(f32[1,32,256]{1,2,0:T(8,128)} %get-tuple-element.1214) | copy-start | bytes 98308 | tf_op jit(solution)/shard_map/transpose(jvp())/while
  404.2 7.7 %copy-start.1 = (f32[32,256]{0,1:T(8,128)S(1)}, f32[32,256]{0,1:T(8,128)}, u32[]{:S(2)}) copy-start(f32[32,256]{0,1:T(8,128)} %get-tuple-element.1215) | copy-start | bytes 98308 | tf_op jit(solution)/shard_map/transpose(jvp())/while
  405.2 13.6 %copy-start.4 = (f32[32,256]{1,0:T(8,128)S(1)}, f32[32,256]{1,0:T(8,128)}, u32[]{:S(2)}) copy-start(f32[32,256]{1,0:T(8,128)} %copy_bitcast_fusion.10) | copy-start | bytes 98308 | tf_op jit(solution)/shard_map/transpose(jvp())/while
  405.2 13.6 %copy-start.15 = (f32[32]{0:T(128)S(1)}, f32[32]{0:T(128)}, u32[]{:S(2)}) copy-start(f32[32]{0:T(128)} %get-tuple-element.1211) | copy-start | bytes 388 | tf_op jit(solution)/shard_map/transpose(jvp())/while
  407.2 11.6 %copy-start = (bf16[256,32,64]{0,2,1:T(8,128)(2,1)S(1)}, bf16[256,32,64]{0,2,1:T(8,128)(2,1)}, u32[]{:S(2)}) copy-start(bf16[256,32,64]{0,2,1:T(8,128)(2,1)} %get-tuple-element.1210) | copy-start | bytes 3145732 | tf_op jit(solution)/shard_map/transpose(jvp())/while
  436.1 8.2 %copy-start.3 = (f32[256,256]{1,0:T(8,128)}, f32[256,256]{1,0:T(8,128)S(1)}, u32[]{:S(2)}) copy-start(f32[256,256]{1,0:T(8,128)S(1)} %fusion.163) | copy-start | bytes 786436 | tf_op jit(solution)/shard_map/transpose(jvp())/while
  454.0 18.4 %copy-start.12 = (f32[32]{0:T(128)S(1)}, f32[32]{0:T(128)}, u32[]{:S(2)}) copy-start(f32[32]{0:T(128)} %fusion.168) | copy-start | bytes 388 | tf_op jit(solution)/shard_map/transpose(jvp())/while
  458.5 7.1 %copy-start.2 = (f32[1,32,256]{1,2,0:T(8,128)S(1)}, f32[1,32,256]{1,2,0:T(8,128)}, u32[]{:S(2)}) copy-start(f32[1,32,256]{1,2,0:T(8,128)} %get-tuple-element.1214) | copy-start | bytes 98308 | tf_op jit(solution)/shard_map/transpose(jvp())/while
  458.5 7.7 %copy-start.1 = (f32[32,256]{0,1:T(8,128)S(1)}, f32[32,256]{0,1:T(8,128)}, u32[]{:S(2)}) copy-start(f32[32,256]{0,1:T(8,128)} %get-tuple-element.1215) | copy-start | bytes 98308 | tf_op jit(solution)/shard_map/transpose(jvp())/while
  459.5 13.6 %copy-start.4 = (f32[32,256]{1,0:T(8,128)S(1)}, f32[32,256]{1,0:T(8,128)}, u32[]{:S(2)}) copy-start(f32[32,256]{1,0:T(8,128)} %copy_bitcast_fusion.10) | copy-start | bytes 98308 | tf_op jit(solution)/shard_map/transpose(jvp())/while
  459.5 13.6 %copy-start.15 = (f32[32]{0:T(128)S(1)}, f32[32]{0:T(128)}, u32[]{:S(2)}) copy-start(f32[32]{0:T(128)} %get-tuple-element.1211) | copy-start | bytes 388 | tf_op jit(solution)/shard_map/transpose(jvp())/while
  461.5 11.6 %copy-start = (bf16[256,32,64]{0,2,1:T(8,128)(2,1)S(1)}, bf16[256,32,64]{0,2,1:T(8,128)(2,1)}, u32[]{:S(2)}) copy-start(bf16[256,32,64]{0,2,1:T(8,128)(2,1)} %get-tuple-element.1210) | copy-start | bytes 3145732 | tf_op jit(solution)/shard_map/transpose(jvp())/while
  490.4 8.2 %copy-start.3 = (f32[256,256]{1,0:T(8,128)}, f32[256,256]{1,0:T(8,128)S(1)}, u32[]{:S(2)}) copy-start(f32[256,256]{1,0:T(8,128)S(1)} %fusion.163) | copy-start | bytes 786436 | tf_op jit(solution)/shard_map/transpose(jvp())/while
  508.2 18.4 %copy-start.12 = (f32[32]{0:T(128)S(1)}, f32[32]{0:T(128)}, u32[]{:S(2)}) copy-start(f32[32]{0:T(128)} %fusion.168) | copy-start | bytes 388 | tf_op jit(solution)/shard_map/transpose(jvp())/while
  512.7 7.1 %copy-start.2 = (f32[1,32,256]{1,2,0:T(8,128)S(1)}, f32[1,32,256]{1,2,0:T(8,128)}, u32[]{:S(2)}) copy-start(f32[1,32,256]{1,2,0:T(8,128)} %get-tuple-element.1214) | copy-start | bytes 98308 | tf_op jit(solution)/shard_map/transpose(jvp())/while
  512.7 7.7 %copy-start.1 = (f32[32,256]{0,1:T(8,128)S(1)}, f32[32,256]{0,1:T(8,128)}, u32[]{:S(2)}) copy-start(f32[32,256]{0,1:T(8,128)} %get-tuple-element.1215) | copy-start | bytes 98308 | tf_op jit(solution)/shard_map/transpose(jvp())/while
  513.7 13.6 %copy-start.4 = (f32[32,256]{1,0:T(8,128)S(1)}, f32[32,256]{1,0:T(8,128)}, u32[]{:S(2)}) copy-start(f32[32,256]{1,0:T(8,128)} %copy_bitcast_fusion.10) | copy-start | bytes 98308 | tf_op jit(solution)/shard_map/transpose(jvp())/while
  513.7 13.6 %copy-start.15 = (f32[32]{0:T(128)S(1)}, f32[32]{0:T(128)}, u32[]{:S(2)}) copy-start(f32[32]{0:T(128)} %get-tuple-element.1211) | copy-start | bytes 388 | tf_op jit(solution)/shard_map/transpose(jvp())/while
  515.7 11.6 %copy-start = (bf16[256,32,64]{0,2,1:T(8,128)(2,1)S(1)}, bf16[256,32,64]{0,2,1:T(8,128)(2,1)}, u32[]{:S(2)}) copy-start(bf16[256,32,64]{0,2,1:T(8,128)(2,1)} %get-tuple-element.1210) | copy-start | bytes 3145732 | tf_op jit(solution)/shard_map/transpose(jvp())/while
  614.1 13.0 %copy-start.6 = (f32[1,32,1024]{2,1,0:T(8,128)S(1)}, f32[1,32,1024]{2,1,0:T(8,128)}, u32[]{:S(2)}) copy-start(f32[1,32,1024]{2,1,0:T(8,128)} %param.19) | copy-start | bytes 393220
  614.1 13.0 %copy-start.11 = (f32[32]{0:T(128)S(1)}, f32[32]{0:T(128)}, u32[]{:S(2)}) copy-start(f32[32]{0:T(128)} %param.20) | copy-start | bytes 388
  614.1 13.0 %copy-start.14 = (f32[32]{0:T(128)S(1)}, f32[32]{0:T(128)}, u32[]{:S(2)}) copy-start(f32[32]{0:T(128)} %copy-done.13) | copy-start | bytes 388
  614.1 13.8 %copy-start.8 = (bf16[4,256,128]{2,1,0:T(8,128)(2,1)S(1)}, bf16[4,256,128]{2,1,0:T(8,128)(2,1)}, u32[]{:S(2)}) copy-start(bf16[4,256,128]{2,1,0:T(8,128)(2,1)} %get-tuple-element.600) | copy-start | bytes 786436
  614.1 13.8 %copy-start.9 = (bf16[4,256,128]{2,1,0:T(8,128)(2,1)S(1)}, bf16[4,256,128]{2,1,0:T(8,128)(2,1)}, u32[]{:S(2)}) copy-start(bf16[4,256,128]{2,1,0:T(8,128)(2,1)} %get-tuple-element.599) | copy-start | bytes 786436
Sparse Core Ops, SparseCore 0:
  33.5 115.2 all-gather.7
  151.0 110.9 all-gather.5
where the time goes:
time: 643 us; the launch traced here: 636 us
  local copies, waits for them, and re-layouts  189 us (29%)
  waiting for transfers between devices  115 us (18%)
  matrix products  108 us (17%)
  other arithmetic  106 us (16%)
  blocking collectives  101 us (16%)
  between operations  14.9 us (2%)
    all_gather x2, waiting for transfers between devices, entering(): everything = jax.tree.map(lambda part: lax.all_gather(part, axis), array)  115 us
    psum x1, blocking collectives, shards(): lax.psum(params, ('seq', 'batch')) * (1.0 / math.sqrt(total_tokens))  64.8 us
    dot_general x8, matrix products, block_step(): jnp.einsum('hts,shp->thp', weights, xc, preferred_element_type=jnp.float32)  51.3 us
    unnamed x30, local copies, waits for them, and re-layouts  50.4 us
    select_n x32, other arithmetic, lap(): return jax.tree.map(lambda a, b: jnp.where(reached, a, b), new, before)  47.2 us
    unnamed x1, blocking collectives  36.4 us
    dot_general x12, matrix products, block_step(): jnp.einsum('shp,sn->hpn', scaled, bc, preferred_element_type=jnp.float32)  31.1 us
    another operation x39, other arithmetic  27.7 us
  transfers between devices with their start and end apart: 2, of which 2 were waited for; matrix products, arithmetic and copies ran while one was open for 12% of the time, Pallas kernels for 0%

commit v1 on v0

v1 whole, which is shorter than its diff:
```python
import functools
import math

import jax
import jax.numpy as jnp
from jax import lax
from jax.experimental import pallas as pl
from jax.experimental.pallas import tpu as pltpu
from jax.sharding import PartitionSpec as P

GROUP = 256
LANES = 128
MESH = pl.DeviceIdType.MESH
BF = jnp.bfloat16
F32 = jnp.float32


def dot(a, b):
    return jnp.dot(a, b, preferred_element_type=F32)


def dot_nt(a, b):
    return lax.dot_general(a, b, (((1,), (1,)), ((), ())), preferred_element_type=F32)


def two_parts(v):
    high = v.astype(BF).astype(F32)
    return high, v - high


def sum_dot(v, ones):
    high, rest = two_parts(v)
    mid, low = two_parts(rest)
    rows = v.shape[0]
    out = dot(jnp.concatenate([high, mid, low], axis=0).astype(BF), ones)
    return out[:rows] + out[rows : 2 * rows] + out[2 * rows :]


def kernel(
    nseq,
    x_hbm,
    dy_hbm,
    b_ref,
    c_ref,
    raw_ref,
    par_ref,
    dx_hbm,
    db_ref,
    dc_ref,
    draw_ref,
    gpar_ref,
    x_buf,
    dy_buf,
    xt_buf,
    dyt_buf,
    fm_buf,
    dxi_buf,
    ds_buf,
    dg_buf,
    ecl_buf,
    step_buf,
    racc_buf,
    send_buf,
    recv_buf,
    back_buf,
    home_buf,
    stb_buf,
    gtb_buf,
    bdot_buf,
    ohp_buf,
    ohm_buf,
    ota_buf,
    otb_buf,
    skip_buf,
    in_sem,
    out_sem,
    s1,
    r1,
    s2,
    r2,
):
    tokens, width = x_buf.shape
    heads = raw_ref.shape[0]
    hs = width // heads
    states = b_ref.shape[1]
    blocks = tokens // GROUP
    gw = min(256, width)
    groups = width // gw
    ow = width // nseq
    me = lax.axis_index("seq")

    def rows_of(b):
        return pl.ds(b * GROUP, GROUP)

    def x_in(b):
        return pltpu.make_async_copy(x_hbm.at[rows_of(b)], x_buf.at[rows_of(b)], in_sem.at[0, b])

    def dy_in(b):
        return pltpu.make_async_copy(dy_hbm.at[rows_of(b)], dy_buf.at[rows_of(b)], in_sem.at[1, b])

    for b in range(blocks):
        x_in(b).start()
        dy_in(b).start()

    bar = pltpu.get_barrier_semaphore()
    for k in range(1, nseq):
        pl.semaphore_signal(
            bar, inc=1, device_id={"seq": lax.rem(me + k, nseq)}, device_id_type=MESH
        )

    k_id = lax.broadcasted_iota(jnp.int32, (LANES, width), 0)
    l_id = lax.broadcasted_iota(jnp.int32, (LANES, width), 1) // hs
    same = (k_id % heads) == l_id
    ohp_buf[...] = jnp.where(same & (k_id < 2 * heads), 1.0, 0.0).astype(BF)
    ohm_buf[...] = jnp.where(same & (k_id >= 2 * heads), 1.0, 0.0).astype(BF)
    j_id = lax.broadcasted_iota(jnp.int32, (width, LANES), 1)
    h_id = lax.broadcasted_iota(jnp.int32, (width, LANES), 0) // hs
    ota_buf[...] = jnp.where(j_id == h_id, 1.0, 0.0).astype(BF)
    otb_buf[...] = jnp.where(j_id == h_id + heads, 1.0, 0.0).astype(BF)

    eye = lax.broadcasted_iota(jnp.int32, (heads, LANES), 0) == lax.broadcasted_iota(
        jnp.int32, (heads, LANES), 1
    )
    head_lane = (
        lax.broadcasted_iota(jnp.int32, (heads, width), 0)
        == lax.broadcasted_iota(jnp.int32, (heads, width), 1) // hs
    )

    def column(row):
        return jnp.sum(jnp.where(eye, row, 0.0), axis=1, keepdims=True)

    def expand(col):
        return jnp.sum(jnp.where(head_lane, col, 0.0), axis=0, keepdims=True)

    def per_head(row):
        return jnp.sum(jnp.where(head_lane, row, 0.0), axis=1, keepdims=True)

    bias = column(par_ref[0:1])
    rate = column(par_ref[1:2])
    skip_row = expand(column(par_ref[2:3]))

    t_id = lax.broadcasted_iota(jnp.int32, (GROUP, GROUP), 0)
    s_id = lax.broadcasted_iota(jnp.int32, (GROUP, GROUP), 1)
    lower = s_id <= t_id
    upper = s_id >= t_id
    ones_le = jnp.where(upper, 1.0, 0.0).astype(BF)
    ones_ge = jnp.where(lower, 1.0, 0.0).astype(BF)

    skip_buf[...] = jnp.zeros_like(skip_buf)
    home_buf[...] = jnp.zeros_like(home_buf)

    def local(b, carry):
        rows = rows_of(b)
        v = raw_ref[:, pl.ds(pl.multiple_of(b * GROUP, GROUP), GROUP)] + bias
        step = jnp.maximum(v, 0.0) + jnp.log1p(jnp.exp(-jnp.abs(v)))
        step_buf[b] = step
        cum = sum_dot(-rate * step, ones_le)
        ep = jnp.exp(cum)
        em = step * jnp.exp(-cum)
        ep_hi, ep_lo = two_parts(ep)
        em_hi, em_lo = two_parts(em)
        parts = jnp.concatenate([ep_hi, ep_lo, em_hi, em_lo], axis=0).T.astype(BF)
        ecl_buf[b] = expand(ep[:, GROUP - 1 : GROUP])
        x_in(b).wait()
        dy_in(b).wait()
        bt = b_ref[rows]
        ct = c_ref[rows]

        def lane_group(g, _):
            lanes = pl.ds(pl.multiple_of(g * gw, gw), gw)
            fp = dot(parts, ohp_buf[:, lanes])
            fm = dot(parts, ohm_buf[:, lanes])
            fm_buf[rows, lanes] = fm
            xg = x_buf[rows, lanes].astype(F32)
            dyg = dy_buf[rows, lanes].astype(F32)
            xt = (xg * fm).astype(BF)
            dyt = (dyg * fp).astype(BF)
            xt_buf[rows, lanes] = xt
            dyt_buf[rows, lanes] = dyt
            prod = xg * dyg
            skip_buf[:, lanes] += jnp.sum(prod.reshape(GROUP // 8, 8, gw), axis=0)
            ds_buf[b, :, lanes] = lax.dot_general(
                bt, xt, (((0,), (0,)), ((), ())), preferred_element_type=F32
            )
            dg_buf[b, :, lanes] = lax.dot_general(
                ct, dyt, (((0,), (0,)), ((), ())), preferred_element_type=F32
            )
            return 0

        lax.fori_loop(0, groups, lane_group, 0)
        return carry

    lax.fori_loop(0, blocks, local, 0)

    for j in range(nseq):
        lanes = slice(j * ow, (j + 1) * ow)
        st = ds_buf[0, :, lanes] * ecl_buf[0, :, lanes]
        gt = dg_buf[0, :, lanes]
        decay = ecl_buf[0, :, lanes]
        for b in range(1, blocks):
            e = ecl_buf[b, :, lanes]
            st = (st + ds_buf[b, :, lanes]) * e
            gt = gt + decay * dg_buf[b, :, lanes]
            decay = decay * e
        send_buf[j, 0:states] = st
        send_buf[j, states : 2 * states] = gt
        send_buf[j, 2 * states :] = jnp.broadcast_to(decay, (8, ow))

    pl.semaphore_wait(bar, nseq - 1)

    def there(k):
        peer = lax.rem(me + k, nseq)
        return pltpu.make_async_remote_copy(
            src_ref=send_buf.at[peer],
            dst_ref=recv_buf.at[me],
            send_sem=s1.at[k],
            recv_sem=r1.at[k],
            device_id={"seq": peer},
            device_id_type=MESH,
        )

    def again(k):
        peer = lax.rem(me + k, nseq)
        return pltpu.make_async_remote_copy(
            src_ref=back_buf.at[peer],
            dst_ref=home_buf.at[me],
            send_sem=s2.at[k],
            recv_sem=r2.at[k],
            device_id={"seq": peer},
            device_id_type=MESH,
        )

    for k in range(1, nseq):
        there(k).start()
    recv_buf[me] = send_buf[me]

    def inside(b, carry):
        rows = rows_of(b)
        bt = b_ref[rows]
        ct = c_ref[rows]
        scores = jnp.where(lower, dot_nt(ct, bt), 0.0).astype(BF)
        flipped = jnp.where(upper, dot_nt(bt, ct), 0.0).astype(BF)

        def lane_group(g, acc):
            lanes = pl.ds(pl.multiple_of(g * gw, gw), gw)
            xt = xt_buf[rows, lanes]
            dyt = dyt_buf[rows, lanes]
            yi = dot(scores, xt)
            dxi = dot(flipped, dyt)
            dxi_buf[rows, lanes] = dxi
            rp = (yi * dyt.astype(F32)).astype(BF)
            cp = (dxi * xt.astype(F32)).astype(BF)
            lane_rows = pl.ds(pl.multiple_of(g * gw, gw), gw)
            racc_buf[rows] += dot(rp, ota_buf[lane_rows]) + dot(cp, otb_buf[lane_rows])
            return acc

        racc_buf[rows] = jnp.zeros((GROUP, LANES), F32)
        lax.fori_loop(0, groups, lane_group, 0)
        ds = jnp.where(lower, dot_nt(dyt_buf[rows], xt_buf[rows]), 0.0)
        dc_ref[rows] = dot(ds.astype(BF), bt)
        db_ref[rows] = dot(ds.T.astype(BF), ct)
        return carry

    lax.fori_loop(0, blocks, inside, 0)

    for k in range(1, nseq):
        there(k).wait()

    st = jnp.zeros((states, ow), F32)
    for i in range(nseq):
        back_buf[i, 0:states] = st
        st = st * recv_buf[i, 2 * states : 2 * states + 1] + recv_buf[i, 0:states]
    gt = jnp.zeros((states, ow), F32)
    for i in reversed(range(nseq)):
        back_buf[i, states : 2 * states] = gt
        gt = (
            gt * recv_buf[i, 2 * states : 2 * states + 1] + recv_buf[i, states : 2 * states]
        )

    for k in range(1, nseq):
        again(k).start()
    home_buf[me] = back_buf[me]
    for k in range(1, nseq):
        again(k).wait()

    for j in range(nseq):
        lanes = slice(j * ow, (j + 1) * ow)
        st = home_buf[j, 0:states]
        ends = []
        for b in range(blocks):
            stb_buf[b, :, lanes] = st.astype(BF)
            st = (st + ds_buf[b, :, lanes]) * ecl_buf[b, :, lanes]
            ends.append(st)
        gt = home_buf[j, states : 2 * states]
        for b in reversed(range(blocks)):
            bdot_buf[b, :, lanes] = jnp.sum(gt * ends[b], axis=0, keepdims=True)
            gt = gt * ecl_buf[b, :, lanes]
            gtb_buf[b, :, lanes] = gt.astype(BF)
            gt = gt + dg_buf[b, :, lanes]

    def dx_out(b):
        return pltpu.make_async_copy(x_buf.at[rows_of(b)], dx_hbm.at[rows_of(b)], out_sem.at[b])

    def finish(b, carry):
        gbias, grate = carry
        rows = rows_of(b)
        bt = b_ref[rows]
        ct = c_ref[rows]

        def lane_group(g, acc):
            lanes = pl.ds(pl.multiple_of(g * gw, gw), gw)
            lane_rows = pl.ds(pl.multiple_of(g * gw, gw), gw)
            yc = dot(ct, stb_buf[b, :, lanes])
            dxc = dot(bt, gtb_buf[b, :, lanes])
            rp = (yc * dyt_buf[rows, lanes].astype(F32)).astype(BF)
            cp = (dxc * xt_buf[rows, lanes].astype(F32)).astype(BF)
            racc_buf[rows] += dot(rp, ota_buf[lane_rows]) + dot(cp, otb_buf[lane_rows])
            skip = skip_row_ref[0:1, lanes]
            dx = fm_buf[rows, lanes] * (dxi_buf[rows, lanes] + dxc) + skip * dy_buf[
                rows, lanes
            ].astype(F32)
            x_buf[rows, lanes] = dx.astype(BF)
            return acc

        lax.fori_loop(0, groups, lane_group, 0)
        dx_out(b).start()
        dc_ref[rows] += dot_nt(dyt_buf[rows], stb_buf[b])
        db_ref[rows] += dot_nt(xt_buf[rows], gtb_buf[b])
        dots = racc_buf[rows].T
        rowdot = dots[0:heads]
        coldot = dots[heads : 2 * heads]
        dlog = sum_dot(rowdot - coldot, ones_ge) + per_head(bdot_buf[b])
        step = step_buf[b]
        cols = pl.ds(pl.multiple_of(b * GROUP, GROUP), GROUP)
        v = raw_ref[:, cols] + bias
        draw = (coldot / step - rate * dlog) / (1.0 + jnp.exp(-v))
        draw_ref[:, cols] = draw
        gbias = gbias + jnp.sum(draw, axis=1, keepdims=True)
        grate = grate - jnp.sum(step * dlog, axis=1, keepdims=True)
        return gbias, grate

    zero = jnp.zeros((heads, 1), F32)
    skip_row_ref = bdot_buf.at[blocks]
    skip_row_ref[...] = skip_row
    gbias, grate = lax.fori_loop(0, blocks, finish, (zero, zero))
    gskip = per_head(jnp.sum(skip_buf[...], axis=0, keepdims=True))
    lane = lax.broadcasted_iota(jnp.int32, (heads, LANES), 1)
    gpar_ref[...] = jnp.where(
        lane == 0, gbias, jnp.where(lane == 1, grate, jnp.where(lane == 2, gskip, 0.0))
    )
    for b in range(blocks):
        dx_out(b).wait()


def shards(inputs, input_map, output_map, step_raw, step_bias, decay_rate, skip_gain, cotangent):
    tokens, width = inputs.shape[1:]
    heads = step_raw.shape[1]
    states = input_map.shape[2]
    nseq = lax.axis_size("seq")
    blocks = tokens // GROUP
    ow = width // nseq
    par = jnp.pad(jnp.stack([step_bias, decay_rate, skip_gain]), ((0, 5), (0, LANES - heads)))
    vmem = pl.BlockSpec(memory_space=pltpu.VMEM)
    hbm = pl.BlockSpec(memory_space=pl.ANY)
    dma = pltpu.SemaphoreType.DMA
    dx, db, dc, draw, gpar = pl.pallas_call(
        functools.partial(kernel, nseq),
        out_shape=(
            jax.ShapeDtypeStruct((tokens, width), BF),
            jax.ShapeDtypeStruct((tokens, states), F32),
            jax.ShapeDtypeStruct((tokens, states), F32),
            jax.ShapeDtypeStruct((heads, tokens), F32),
            jax.ShapeDtypeStruct((heads, LANES), F32),
        ),
        in_specs=[hbm, hbm, vmem, vmem, vmem, vmem],
        out_specs=(hbm, vmem, vmem, vmem, vmem),
        scratch_shapes=[
            pltpu.VMEM((tokens, width), BF),
            pltpu.VMEM((tokens, width), BF),
            pltpu.VMEM((tokens, width), BF),
            pltpu.VMEM((tokens, width), BF),
            pltpu.VMEM((tokens, width), F32),
            pltpu.VMEM((tokens, width), F32),
            pltpu.VMEM((blocks, states, width), F32),
            pltpu.VMEM((blocks, states, width), F32),
            pltpu.VMEM((blocks, 1, width), F32),
            pltpu.VMEM((blocks, heads, GROUP), F32),
            pltpu.VMEM((tokens, LANES), F32),
            pltpu.VMEM((nseq, 2 * states + 8, ow), F32),
            pltpu.VMEM((nseq, 2 * states + 8, ow), F32),
            pltpu.VMEM((nseq, 2 * states, ow), F32),
            pltpu.VMEM((nseq, 2 * states, ow), F32),
            pltpu.VMEM((blocks, states, width), BF),
            pltpu.VMEM((blocks, states, width), BF),
            pltpu.VMEM((blocks + 1, 1, width), F32),
            pltpu.VMEM((LANES, width), BF),
            pltpu.VMEM((LANES, width), BF),
            pltpu.VMEM((width, LANES), BF),
            pltpu.VMEM((width, LANES), BF),
            pltpu.VMEM((8, width), F32),
            dma((2, blocks)),
            dma((blocks,)),
            dma((nseq,)),
            dma((nseq,)),
            dma((nseq,)),
            dma((nseq,)),
        ],
        compiler_params=pltpu.CompilerParams(
            collective_id=0, has_side_effects=True, vmem_limit_bytes=62 << 20
        ),
    )(inputs[0], cotangent[0], input_map[0], output_map[0], step_raw[0], par)
    total_tokens = tokens * nseq * lax.axis_size("batch")
    summed = lax.psum(gpar[:, 0:3].T, ("seq", "batch")) * (1.0 / math.sqrt(total_tokens))
    pair = jnp.stack([summed[0], summed[2]])
    return dx[None], db[None], dc[None], draw[None], pair, summed[1]


def solution(mesh):
    in_specs = (
        P("batch", "seq", None),
        P("batch", "seq", None),
        P("batch", "seq", None),
        P("batch", None, "seq"),
        P(),
        P(),
        P(),
        P("batch", "seq", None),
    )
    out_specs = (
        P("batch", "seq", None),
        P("batch", "seq", None),
        P("batch", "seq", None),
        P("batch", None, "seq"),
        P(),
        P(),
    )
    return jax.shard_map(shards, mesh=mesh, in_specs=in_specs, out_specs=out_specs, check_vma=False)
```

time: 643 us -> 184 us (0.29); the launches traced: 636 us -> 184 us
  local copies, waits for them, and re-layouts: 189 us -> 8.7 us
  waiting for transfers between devices: 115 us -> 0 us
  matrix products: 108 us -> 0 us
  other arithmetic: 106 us -> 1.88 us
  Pallas kernels: 0 us -> 99.5 us
  blocking collectives: 101 us -> 73.4 us
  between operations: 14.9 us -> 0.65 us
    all_gather x2 -> x0, waiting for transfers between devices: 115 us -> none  [entering(): everything = jax.tree.map(lambda part: lax.all_gather(part, axis), array)]
    dot_general x46 -> x0, matrix products: 108 us -> none  [the longest x8 51.3 us: block_step(): jnp.einsum('hts,shp->thp', weights, xc, preferred_element_type=jnp.float32)]
    pallas_call x0 -> x1, Pallas kernels: none -> 99.5 us  [shards(): pl.pallas_call(functools.partial(kernel, nseq), out_shape=(jax.ShapeDtype...]
    select_n x32 -> x0, other arithmetic: 47.2 us -> none  [lap(): return jax.tree.map(lambda a, b: jnp.where(reached, a, b), new, before)]
    unnamed x30 -> x10, local copies, waits for them, and re-layouts: 50.4 us -> 7.14 us
    unnamed x1 -> x0, blocking collectives: 36.4 us -> none
    another operation x50 -> x0, local copies, waits for them, and re-layouts: 31.6 us -> none  [the longest x1 12.9 us: scan_forward(): return (outs.reshape(length, heads, head_size), end_state)]
    reduce_sum x20 -> x0, local copies, waits for them, and re-layouts: 27 us -> none  [the longest x8 12 us: block_step(): gap = jnp.where(lower[None], cum[:, :, None] - cum[:, None, :], -1e+30)]
  transfers between devices with their start and end apart: 2 -> 0, of which waited for: 2 -> 0; matrix products, arithmetic and copies ran while one was open for 12% -> 0% of each run, Pallas kernels for 0% -> 0%
where the time goes in v1:
time: 184 us
  Pallas kernels  99.5 us (54%)
  blocking collectives  73.4 us (40%)
  local copies, waits for them, and re-layouts  8.7 us (5%)
  other arithmetic  1.88 us (1%)
    pallas_call x1, Pallas kernels, shards(): pl.pallas_call(functools.partial(kernel, nseq), out_shape=(jax.ShapeDtype...  99.5 us
    psum x1, blocking collectives, shards(): lax.psum(gpar[:, 0:3].T, ('seq', 'batch')) * (1.0 / math.sqrt(total_tokens))  73.4 us
    unnamed x10, local copies, waits for them, and re-layouts  7.14 us

profile of v1, /device:TPU:1, one launch (start us, length us, event | category | flops | bytes accessed | tf_op | source)
XLA Modules:
  0.0 184.1 jit_solution(9323847619299797708)
XLA Ops:
  0.6 1.3 select_maximum_fusion.par_ref
  1.9 99.5 %shard_map.127 = (bf16[1024,2048]{1,0:T(8,128)(2,1)}, f32[1024,128]{1,0:T(8,128)}, f32[1024,128]{1,0:T(8,128)}, f32[32,1024]{1,0:T(8,128)}, f32[32,128]{1,0:T(8,128)}) custom-call(bf16[1024,2048]{1,0:T(8,128)(2,1)} %bitcast.14, bf16[1024,2048]{1,0:T(8,128)(2,1)} %bitcast.15, bf16[1024,128]{1,0:T(8,128)(2,1)} %bitcast.19, bf16[1024,128]{1,0:T(8,128)(2,1)} %bitcast.20, ...), custom_call_target="tpu_custom_call" | custom-call | tf_op jit(solution)/shard_map/pallas_call | solution.py:366
  101.4 0.7 slice_bitcast_fusion
  102.1 73.4 %psum.7 = f32[3,32]{0,1:T(8,128)S(1)} all-reduce(f32[3,32]{0,1:T(8,128)S(1)} %slice_bitcast_fusion), channel_id=1, replica_groups=mesh['seq'=16,'batch'=8] {'seq','batch'}, use_global_device_ids=true, to_apply=%region_0.1 | all-reduce | flops 96 | bytes 768 | tf_op jit(solution)/shard_map/psum | solution.py:413
  175.6 0.7 slice_reduce_fusion
  176.2 0.1 copy.16
  176.3 0.1 copy.17
  176.4 0.6 pad_maximum_fusion
  177.0 0.0 copy-start.1
  177.0 0.0 copy-start
  177.0 0.0 copy-start.2
  177.0 4.9 %copy.22 = bf16[1,1024,2048]{2,1,0:T(8,128)(2,1)} copy(bf16[1,1024,2048]{2,1,0:T(8,128)(2,1)} %bitcast.16) | data formatting | bytes 8388608
  181.9 0.0 copy-done.1
  181.9 0.8 copy.23
  182.7 0.0 copy-done
  182.7 0.8 copy.24
  183.5 0.0 copy-done.2
  183.5 0.7 copy.25
  (1 shorter events, 0.0 us)
Async XLA Ops:
  177.0 4.9 %copy-start.1 = (f32[1024,128]{1,0:T(8,128)S(1)}, f32[1024,128]{1,0:T(8,128)}, u32[]{:S(2)}) copy-start(f32[1024,128]{1,0:T(8,128)} %get-tuple-element.12) | copy-start | bytes 1572868
  177.0 5.7 %copy-start = (f32[1024,128]{1,0:T(8,128)S(1)}, f32[1024,128]{1,0:T(8,128)}, u32[]{:S(2)}) copy-start(f32[1024,128]{1,0:T(8,128)} %get-tuple-element.13) | copy-start | bytes 1572868
  177.0 6.5 %copy-start.2 = (f32[32,1024]{1,0:T(8,128)S(1)}, f32[32,1024]{1,0:T(8,128)}, u32[]{:S(2)}) copy-start(f32[32,1024]{1,0:T(8,128)} %get-tuple-element.14) | copy-start | bytes 393220

commit v2 on v1

--- a/solution.py
+++ b/solution.py
@@ -38,6 +38,8 @@
 
 def kernel(
     nseq,
+    nbatch,
+    scale,
     x_hbm,
     dy_hbm,
     b_ref,
@@ -78,6 +80,13 @@
     r1,
     s2,
     r2,
+    p1_buf,
+    p2_buf,
+    mine_buf,
+    s3,
+    r3,
+    s4,
+    r4,
 ):
     tokens, width = x_buf.shape
     heads = raw_ref.shape[0]
@@ -88,6 +97,7 @@
     groups = width // gw
     ow = width // nseq
     me = lax.axis_index("seq")
+    my_batch = lax.axis_index("batch")
 
     def rows_of(b):
         return pl.ds(b * GROUP, GROUP)
@@ -106,6 +116,10 @@
     for k in range(1, nseq):
         pl.semaphore_signal(
             bar, inc=1, device_id={"seq": lax.rem(me + k, nseq)}, device_id_type=MESH
+        )
+    for k in range(1, nbatch):
+        pl.semaphore_signal(
+            bar, inc=1, device_id={"batch": lax.rem(my_batch + k, nbatch)}, device_id_type=MESH
         )
 
     k_id = lax.broadcasted_iota(jnp.int32, (LANES, width), 0)
@@ -206,7 +220,7 @@
         send_buf[j, states : 2 * states] = gt
         send_buf[j, 2 * states :] = jnp.broadcast_to(decay, (8, ow))
 
-    pl.semaphore_wait(bar, nseq - 1)
+    pl.semaphore_wait(bar, nseq + nbatch - 2)
 
     def there(k):
         peer = lax.rem(me + k, nseq)
@@ -344,10 +358,54 @@
     skip_row_ref[...] = skip_row
     gbias, grate = lax.fori_loop(0, blocks, finish, (zero, zero))
     gskip = per_head(jnp.sum(skip_buf[...], axis=0, keepdims=True))
-    lane = lax.broadcasted_iota(jnp.int32, (heads, LANES), 1)
-    gpar_ref[...] = jnp.where(
-        lane == 0, gbias, jnp.where(lane == 1, grate, jnp.where(lane == 2, gskip, 0.0))
+
+    def row(col):
+        return jnp.sum(jnp.where(eye, col, 0.0), axis=0, keepdims=True)
+
+    mine_buf[0] = jnp.concatenate(
+        [row(gbias), row(gskip), row(grate), jnp.zeros((5, LANES), F32)], axis=0
     )
+
+    def over_seq(k):
+        peer = lax.rem(me + k, nseq)
+        return pltpu.make_async_remote_copy(
+            src_ref=mine_buf.at[0],
+            dst_ref=p1_buf.at[me],
+            send_sem=s3.at[k],
+            recv_sem=r3.at[k],
+            device_id={"seq": peer},
+            device_id_type=MESH,
+        )
+
+    def over_batch(k):
+        peer = lax.rem(my_batch + k, nbatch)
+        return pltpu.make_async_remote_copy(
+            src_ref=mine_buf.at[1],
+            dst_ref=p2_buf.at[my_batch],
+            send_sem=s4.at[k],
+            recv_sem=r4.at[k],
+            device_id={"batch": peer},
+            device_id_type=MESH,
+        )
+
+    for k in range(1, nseq):
+        over_seq(k).start()
+    p1_buf[me] = mine_buf[0]
+    for k in range(1, nseq):
+        over_seq(k).wait()
+    total = p1_buf[0]
+    for i in range(1, nseq):
+        total = total + p1_buf[i]
+    mine_buf[1] = total
+    for k in range(1, nbatch):
+        over_batch(k).start()
+    p2_buf[my_batch] = total
+    for k in range(1, nbatch):
+        over_batch(k).wait()
+    total = p2_buf[0]
+    for i in range(1, nbatch):
+        total = total + p2_buf[i]
+    gpar_ref[...] = total * scale
     for b in range(blocks):
         dx_out(b).wait()
 
@@ -357,6 +415,7 @@
     heads = step_raw.shape[1]
     states = input_map.shape[2]
     nseq = lax.axis_size("seq")
+    nbatch = lax.axis_size("batch")
     blocks = tokens // GROUP
     ow = width // nseq
     par = jnp.pad(jnp.stack([step_bias, decay_rate, skip_gain]), ((0, 5), (0, LANES - heads)))
@@ -364,13 +423,13 @@
     hbm = pl.BlockSpec(memory_space=pl.ANY)
     dma = pltpu.SemaphoreType.DMA
     dx, db, dc, draw, gpar = pl.pallas_call(
-        functools.partial(kernel, nseq),
+        functools.partial(kernel, nseq, nbatch, 1.0 / math.sqrt(tokens * nseq * nbatch)),
         out_shape=(
             jax.ShapeDtypeStruct((tokens, width), BF),
             jax.ShapeDtypeStruct((tokens, states), F32),
             jax.ShapeDtypeStruct((tokens, states), F32),
             jax.ShapeDtypeStruct((heads, tokens), F32),
-            jax.ShapeDtypeStruct((heads, LANES), F32),
+            jax.ShapeDtypeStruct((8, LANES), F32),
         ),
         in_specs=[hbm, hbm, vmem, vmem, vmem, vmem],
         out_specs=(hbm, vmem, vmem, vmem, vmem),
@@ -404,15 +463,19 @@
             dma((nseq,)),
             dma((nseq,)),
             dma((nseq,)),
+            pltpu.VMEM((nseq, 8, LANES), F32),
+            pltpu.VMEM((nbatch, 8, LANES), F32),
+            pltpu.VMEM((2, 8, LANES), F32),
+            dma((nseq,)),
+            dma((nseq,)),
+            dma((nbatch,)),
+            dma((nbatch,)),
         ],
         compiler_params=pltpu.CompilerParams(
             collective_id=0, has_side_effects=True, vmem_limit_bytes=62 << 20
         ),
     )(inputs[0], cotangent[0], input_map[0], output_map[0], step_raw[0], par)
-    total_tokens = tokens * nseq * lax.axis_size("batch")
-    summed = lax.psum(gpar[:, 0:3].T, ("seq", "batch")) * (1.0 / math.sqrt(total_tokens))
-    pair = jnp.stack([summed[0], summed[2]])
-    return dx[None], db[None], dc[None], draw[None], pair, summed[1]
+    return dx[None], db[None], dc[None], draw[None], gpar[0:2, 0:heads], gpar[2, 0:heads]
 
 
 def solution(mesh):

time: 184 us -> 133 us (0.72)
  blocking collectives: 73.4 us -> 0 us
  Pallas kernels: 99.5 us -> 121 us
    psum x1 -> x0, blocking collectives: 73.4 us -> none  [shards(): lax.psum(gpar[:, 0:3].T, ('seq', 'batch')) * (1.0 / math.sqrt(total_tokens))]
    pallas_call x1, Pallas kernels: 99.5 us -> 121 us  [shards(): pl.pallas_call(functools.partial(kernel, nseq, nbatch, 1.0 / math.sqrt(to...]
where the time goes in v2:
time: 133 us
  Pallas kernels  121 us (91%)
  local copies, waits for them, and re-layouts  9.57 us (7%)
    pallas_call x1, Pallas kernels, shards(): pl.pallas_call(functools.partial(kernel, nseq, nbatch, 1.0 / math.sqrt(to...  121 us
    unnamed x10, local copies, waits for them, and re-layouts  7.14 us

profile of v2, /device:TPU:1, one launch (start us, length us, event | category | flops | bytes accessed | tf_op | source)
XLA Modules:
  0.0 132.6 jit_solution(4918337452618142527)
XLA Ops:
  0.6 1.3 select_maximum_fusion.par_ref
  1.9 121.1 %shard_map.127 = (bf16[1024,2048]{1,0:T(8,128)(2,1)}, f32[1024,128]{1,0:T(8,128)}, f32[1024,128]{1,0:T(8,128)}, f32[32,1024]{1,0:T(8,128)}, f32[8,128]{1,0:T(8,128)}) custom-call(bf16[1024,2048]{1,0:T(8,128)(2,1)} %bitcast.14, bf16[1024,2048]{1,0:T(8,128)(2,1)} %bitcast.15, bf16[1024,128]{1,0:T(8,128)(2,1)} %bitcast.19, bf16[1024,128]{1,0:T(8,128)(2,1)} %bitcast.20, ...), custom_call_target="tpu_custom_call" | custom-call | tf_op jit(solution)/shard_map/pallas_call | solution.py:425
  123.1 1.2 slice.6
  124.3 1.2 slice_bitcast_fusion
  125.5 0.0 copy-start.1
  125.5 0.0 copy-start
  125.5 0.0 copy-start.2
  125.5 4.9 %copy.18 = bf16[1,1024,2048]{2,1,0:T(8,128)(2,1)} copy(bf16[1,1024,2048]{2,1,0:T(8,128)(2,1)} %bitcast.16) | data formatting | bytes 8388608
  130.4 0.0 copy-done.1
  130.4 0.8 copy.19
  131.2 0.0 copy-done
  131.2 0.8 copy.20
  132.0 0.0 copy-done.2
  132.0 0.7 copy.21
Async XLA Ops:
  125.5 4.9 %copy-start.1 = (f32[1024,128]{1,0:T(8,128)S(1)}, f32[1024,128]{1,0:T(8,128)}, u32[]{:S(2)}) copy-start(f32[1024,128]{1,0:T(8,128)} %get-tuple-element.12) | copy-start | bytes 1572868
  125.5 5.7 %copy-start = (f32[1024,128]{1,0:T(8,128)S(1)}, f32[1024,128]{1,0:T(8,128)}, u32[]{:S(2)}) copy-start(f32[1024,128]{1,0:T(8,128)} %get-tuple-element.13) | copy-start | bytes 1572868
  125.5 6.5 %copy-start.2 = (f32[32,1024]{1,0:T(8,128)S(1)}, f32[32,1024]{1,0:T(8,128)}, u32[]{:S(2)}) copy-start(f32[32,1024]{1,0:T(8,128)} %get-tuple-element.14) | copy-start | bytes 393220

commit v3 on v2

v3 whole, which is shorter than its diff:
```python
import functools
import math

import jax
import jax.numpy as jnp
from jax import lax
from jax.experimental import pallas as pl
from jax.experimental.pallas import tpu as pltpu
from jax.sharding import PartitionSpec as P

GROUP = 256
LANES = 128
PARTS = 4
MESH = pl.DeviceIdType.MESH
BF = jnp.bfloat16
F32 = jnp.float32


def dot(a, b):
    return jnp.dot(a, b, preferred_element_type=F32)


def dot_nt(a, b):
    return lax.dot_general(a, b, (((1,), (1,)), ((), ())), preferred_element_type=F32)


def two_parts(v):
    high = v.astype(BF).astype(F32)
    return high, v - high


def sum_dot(v, ones):
    high, rest = two_parts(v)
    mid, low = two_parts(rest)
    rows = v.shape[0]
    out = dot(jnp.concatenate([high, mid, low], axis=0).astype(BF), ones)
    return out[:rows] + out[rows : 2 * rows] + out[2 * rows :]


def kernel(
    nseq,
    nbatch,
    parts,
    scale,
    x_hbm,
    dy_hbm,
    b_ref,
    c_ref,
    raw_ref,
    par_ref,
    dx_hbm,
    db_ref,
    dc_ref,
    draw_ref,
    gpar_ref,
    x_buf,
    dy_buf,
    dyt_buf,
    fm_buf,
    dxp_buf,
    ds_buf,
    dg_buf,
    ecl_buf,
    step_buf,
    fac_buf,
    bt_buf,
    ct_buf,
    low_buf,
    up_buf,
    dsm_buf,
    rc_buf,
    racc_buf,
    send_buf,
    recv_buf,
    back_buf,
    home_buf,
    stb_buf,
    gtb_buf,
    bdot_buf,
    ohp_buf,
    ohm_buf,
    ot_buf,
    skip_buf,
    skiprow_buf,
    dec_buf,
    decs_buf,
    decx_buf,
    p1_buf,
    p2_buf,
    mine_buf,
    in_sem,
    out_sem,
    s0,
    r0,
    s1,
    r1,
    s2,
    r2,
    s3,
    r3,
    s4,
    r4,
):
    tokens, width = x_buf.shape
    heads = raw_ref.shape[0]
    hs = width // heads
    states = b_ref.shape[1]
    blocks = tokens // GROUP
    pw = width // parts
    gw = min(256, pw)
    groups = pw // gw
    rn = states // nseq
    chunk = max(rn, 16)
    me = lax.axis_index("seq")
    my_batch = lax.axis_index("batch")

    def rows_of(b):
        return pl.ds(pl.multiple_of(b * GROUP, GROUP), GROUP)

    def x_in(b):
        return pltpu.make_async_copy(x_hbm.at[rows_of(b)], x_buf.at[rows_of(b)], in_sem.at[0, b])

    def dy_in(b):
        return pltpu.make_async_copy(dy_hbm.at[rows_of(b)], dy_buf.at[rows_of(b)], in_sem.at[1, b])

    for b in range(blocks):
        x_in(b).start()
        dy_in(b).start()

    bar = pltpu.get_barrier_semaphore()
    for k in range(1, nseq):
        pl.semaphore_signal(
            bar, inc=1, device_id={"seq": lax.rem(me + k, nseq)}, device_id_type=MESH
        )
    for k in range(1, nbatch):
        pl.semaphore_signal(
            bar, inc=1, device_id={"batch": lax.rem(my_batch + k, nbatch)}, device_id_type=MESH
        )

    k_id = lax.broadcasted_iota(jnp.int32, (LANES, width), 0)
    l_id = lax.broadcasted_iota(jnp.int32, (LANES, width), 1) // hs
    same = (k_id % heads) == l_id
    ohp_buf[...] = jnp.where(same & (k_id < 2 * heads), 1.0, 0.0).astype(BF)
    ohm_buf[...] = jnp.where(same & (k_id >= 2 * heads), 1.0, 0.0).astype(BF)
    j_id = lax.broadcasted_iota(jnp.int32, (pw, LANES), 1)
    h_id = lax.broadcasted_iota(jnp.int32, (pw, LANES), 0) // hs
    for q in range(parts):
        h_q = h_id + q * (pw // hs)
        ot_buf[q, 0:pw] = jnp.where(j_id == h_q, 1.0, 0.0).astype(BF)
        ot_buf[q, pw:] = jnp.where(j_id == h_q + heads, 1.0, 0.0).astype(BF)

    eye = lax.broadcasted_iota(jnp.int32, (heads, LANES), 0) == lax.broadcasted_iota(
        jnp.int32, (heads, LANES), 1
    )
    head_lane = (
        lax.broadcasted_iota(jnp.int32, (heads, width), 0)
        == lax.broadcasted_iota(jnp.int32, (heads, width), 1) // hs
    )

    def column(row):
        return jnp.sum(jnp.where(eye, row, 0.0), axis=1, keepdims=True)

    def row(col):
        return jnp.sum(jnp.where(eye, col, 0.0), axis=0, keepdims=True)

    def expand(col):
        return jnp.sum(jnp.where(head_lane, col, 0.0), axis=0, keepdims=True)

    def per_head(line):
        return jnp.sum(jnp.where(head_lane, line, 0.0), axis=1, keepdims=True)

    bias = column(par_ref[0:1])
    rate = column(par_ref[1:2])
    skiprow_buf[...] = expand(column(par_ref[2:3]))

    t_id = lax.broadcasted_iota(jnp.int32, (GROUP, GROUP), 0)
    s_id = lax.broadcasted_iota(jnp.int32, (GROUP, GROUP), 1)
    lower = s_id <= t_id
    upper = s_id >= t_id
    ones_le = jnp.where(upper, 1.0, 0.0).astype(BF)
    ones_ge = jnp.where(lower, 1.0, 0.0).astype(BF)

    skip_buf[...] = jnp.zeros_like(skip_buf)
    home_buf[...] = jnp.zeros_like(home_buf)

    def factors(b, total):
        v = raw_ref[:, rows_of(b)] + bias
        step = jnp.maximum(v, 0.0) + jnp.log1p(jnp.exp(-jnp.abs(v)))
        step_buf[b] = step
        cum = sum_dot(-rate * step, ones_le)
        ep = jnp.exp(cum)
        em = step * jnp.exp(-cum)
        ep_hi, ep_lo = two_parts(ep)
        em_hi, em_lo = two_parts(em)
        fac_buf[b] = jnp.concatenate([ep_hi, ep_lo, em_hi, em_lo], axis=0).T.astype(BF)
        ecl_buf[b] = expand(ep[:, GROUP - 1 : GROUP])
        bt_buf[b] = b_ref[rows_of(b)].astype(F32).T.astype(BF)
        ct_buf[b] = c_ref[rows_of(b)].astype(F32).T.astype(BF)
        return total * ep[:, GROUP - 1 : GROUP]

    total = lax.fori_loop(0, blocks, factors, jnp.ones((heads, 1), F32))
    dec_buf[...] = jnp.broadcast_to(row(total), (8, LANES))

    def local(q):
        def one_block(b, carry):
            rows = rows_of(b)
            if q == 0:
                x_in(b).wait()
                dy_in(b).wait()
            fac = fac_buf[b]
            bt = bt_buf[b]
            ct = ct_buf[b]
            for g in range(groups):
                lanes = slice(q * pw + g * gw, q * pw + (g + 1) * gw)
                fp = dot(fac, ohp_buf[:, lanes])
                fm = dot(fac, ohm_buf[:, lanes])
                fm_buf[rows, lanes] = fm
                xg = x_buf[rows, lanes].astype(F32)
                dyg = dy_buf[rows, lanes].astype(F32)
                xt = (xg * fm).astype(BF)
                dyt = (dyg * fp).astype(BF)
                x_buf[rows, lanes] = xt
                dyt_buf[rows, lanes] = dyt
                prod = xg * dyg
                skip_buf[:, lanes] += jnp.sum(prod.reshape(GROUP // 8, 8, gw), axis=0)
                ds_buf[b, :, lanes] = dot(bt, xt)
                dg_buf[b, :, lanes] = dot(ct, dyt)
            return carry

        lax.fori_loop(0, blocks, one_block, 0)
        lanes = slice(q * pw, (q + 1) * pw)
        for j in range(nseq):
            n = slice(j * rn, (j + 1) * rn)
            st = ds_buf[0, n, lanes] * ecl_buf[0, :, lanes]
            gt = dg_buf[0, n, lanes]
            decay = ecl_buf[0, :, lanes]
            for b in range(1, blocks):
                e = ecl_buf[b, :, lanes]
                st = (st + ds_buf[b, n, lanes]) * e
                gt = gt + decay * dg_buf[b, n, lanes]
                decay = decay * e
            send_buf[q, j, 0:rn] = st
            send_buf[q, j, rn:] = gt

    def decays(k):
        peer = lax.rem(me + k, nseq)
        return pltpu.make_async_remote_copy(
            src_ref=dec_buf,
            dst_ref=decs_buf.at[me],
            send_sem=s0.at[k],
            recv_sem=r0.at[k],
            device_id={"seq": peer},
            device_id_type=MESH,
        )

    def there(q, k):
        peer = lax.rem(me + k, nseq)
        return pltpu.make_async_remote_copy(
            src_ref=send_buf.at[q, peer],
            dst_ref=recv_buf.at[q, me],
            send_sem=s1.at[q, k],
            recv_sem=r1.at[q, k],
            device_id={"seq": peer},
            device_id_type=MESH,
        )

    def again(q, k):
        peer = lax.rem(me + k, nseq)
        return pltpu.make_async_remote_copy(
            src_ref=back_buf.at[q, peer],
            dst_ref=home_buf.at[q, me],
            send_sem=s2.at[q, k],
            recv_sem=r2.at[q, k],
            device_id={"seq": peer},
            device_id_type=MESH,
        )

    def scores(b, carry):
        bb = b_ref[rows_of(b)]
        cc = c_ref[rows_of(b)]
        low_buf[b] = jnp.where(lower, dot_nt(cc, bb), 0.0).astype(BF)
        up_buf[b] = jnp.where(upper, dot_nt(bb, cc), 0.0).astype(BF)
        return carry

    def inside(q):
        def one_block(b, carry):
            rows = rows_of(b)
            low = low_buf[b]
            up = up_buf[b]
            for g in range(groups):
                lanes = slice(q * pw + g * gw, q * pw + (g + 1) * gw)
                xt = x_buf[rows, lanes]
                dyt = dyt_buf[rows, lanes]
                yi = dot(low, xt)
                dxi = dot(up, dyt)
                rc_buf[:, g * gw : (g + 1) * gw] = (yi * dyt.astype(F32)).astype(BF)
                rc_buf[:, pw + g * gw : pw + (g + 1) * gw] = (dxi * xt.astype(F32)).astype(BF)
                dxp_buf[rows, lanes] = fm_buf[rows, lanes] * dxi + skiprow_buf[
                    :, lanes
                ] * dy_buf[rows, lanes].astype(F32)
            red = dot(rc_buf[...], ot_buf[q])
            lanes = slice(q * pw, (q + 1) * pw)
            ds = dot_nt(dyt_buf[rows, lanes], x_buf[rows, lanes])
            if q > 0:
                red = red + racc_buf[rows]
                ds = ds + dsm_buf[b]
            racc_buf[rows] = red
            if q < parts - 1:
                dsm_buf[b] = ds
            else:
                ds = jnp.where(lower, ds, 0.0)
                dc_ref[rows] = dot(ds.astype(BF), b_ref[rows])
                db_ref[rows] = dot(ds.T.astype(BF), c_ref[rows])
            return carry

        lax.fori_loop(0, blocks, one_block, 0)

    def scan(q):
        lanes = slice(q * pw, (q + 1) * pw)
        for k in range(1, nseq):
            there(q, k).wait()
        st = jnp.zeros((rn, pw), F32)
        gt = jnp.zeros((rn, pw), F32)
        for i in range(nseq):
            back_buf[q, i, 0:rn] = st
            st = st * decx_buf[i : i + 1, lanes] + recv_buf[q, i, 0:rn]
            h = nseq - 1 - i
            back_buf[q, h, rn:] = gt
            gt = gt * decx_buf[h : h + 1, lanes] + recv_buf[q, h, rn:]
        for k in range(1, nseq):
            again(q, k).start()
        home_buf[q, me] = back_buf[q, me]

    def entering(q):
        lanes = slice(q * pw, (q + 1) * pw)
        for k in range(1, nseq):
            again(q, k).wait()
        dots = [jnp.zeros((8, pw), F32) for _ in range(blocks)]
        for i in range(states // chunk):
            n = slice(i * chunk, (i + 1) * chunk)
            js = range(i * chunk // rn, (i + 1) * chunk // rn)
            st = jnp.concatenate([home_buf[q, j, 0:rn] for j in js], axis=0)
            ends = []
            for b in range(blocks):
                stb_buf[b, n, lanes] = st.astype(BF)
                st = (st + ds_buf[b, n, lanes]) * ecl_buf[b, :, lanes]
                ends.append(st)
            gt = jnp.concatenate([home_buf[q, j, rn:] for j in js], axis=0)
            for b in reversed(range(blocks)):
                prod = gt * ends[b]
                dots[b] = dots[b] + jnp.sum(prod.reshape(chunk // 8, 8, pw), axis=0)
                gt = gt * ecl_buf[b, :, lanes]
                gtb_buf[b, n, lanes] = gt.astype(BF)
                gt = gt + dg_buf[b, n, lanes]
        for b in range(blocks):
            bdot_buf[b, :, lanes] = dots[b]

    def dx_out(q, b):
        lanes = slice(q * pw, (q + 1) * pw)
        return pltpu.make_async_copy(
            dy_buf.at[rows_of(b), lanes], dx_hbm.at[rows_of(b), lanes], out_sem.at[q, b]
        )

    def finish(q):
        def one_block(b, carry):
            rows = rows_of(b)
            bb = b_ref[rows]
            cc = c_ref[rows]
            for g in range(groups):
                lanes = slice(q * pw + g * gw, q * pw + (g + 1) * gw)
                yc = dot(cc, stb_buf[b, :, lanes])
                dxc = dot(bb, gtb_buf[b, :, lanes])
                rc_buf[:, g * gw : (g + 1) * gw] = (
                    yc * dyt_buf[rows, lanes].astype(F32)
                ).astype(BF)
                rc_buf[:, pw + g * gw : pw + (g + 1) * gw] = (
                    dxc * x_buf[rows, lanes].astype(F32)
                ).astype(BF)
                dx = fm_buf[rows, lanes] * dxc + dxp_buf[rows, lanes]
                dy_buf[rows, lanes] = dx.astype(BF)
            dx_out(q, b).start()
            lanes = slice(q * pw, (q + 1) * pw)
            red = racc_buf[rows] + dot(rc_buf[...], ot_buf[q])
            dc_ref[rows] += dot_nt(dyt_buf[rows, lanes], stb_buf[b, :, lanes])
            db_ref[rows] += dot_nt(x_buf[rows, lanes], gtb_buf[b, :, lanes])
            if q < parts - 1:
                racc_buf[rows] = red
                return carry
            gbias, grate = carry
            dots = red.T
            rowdot = dots[0:heads]
            coldot = dots[heads : 2 * heads]
            ends = per_head(jnp.sum(bdot_buf[b], axis=0, keepdims=True))
            dlog = sum_dot(rowdot - coldot, ones_ge) + ends
            step = step_buf[b]
            v = raw_ref[:, rows] + bias
            draw = (coldot / step - rate * dlog) / (1.0 + jnp.exp(-v))
            draw_ref[:, rows] = draw
            gbias = gbias + jnp.sum(draw, axis=1, keepdims=True)
            grate = grate - jnp.sum(step * dlog, axis=1, keepdims=True)
            return gbias, grate

        zero = jnp.zeros((heads, 1), F32)
        return lax.fori_loop(0, blocks, one_block, (zero, zero))

    for q in range(parts):
        local(q)
        if q == 0:
            pl.semaphore_wait(bar, nseq + nbatch - 2)
            for k in range(1, nseq):
                decays(k).start()
            decs_buf[me] = dec_buf[...]
        for k in range(1, nseq):
            there(q, k).start()
        recv_buf[q, me] = send_buf[q, me]

    lax.fori_loop(0, blocks, scores, 0)
    for q in range(parts):
        inside(q)
        if q == 0:
            for k in range(1, nseq):
                decays(k).wait()
            every = jnp.concatenate([decs_buf[i, 0:1] for i in range(nseq)], axis=0)
            high, rest = two_parts(every)
            mid, low = two_parts(rest)
            decx_buf[...] = (
                dot(high.astype(BF), ohp_buf[...])
                + dot(mid.astype(BF), ohp_buf[...])
                + dot(low.astype(BF), ohp_buf[...])
            )
        scan(q)

    for q in range(parts):
        entering(q)
        gbias, grate = finish(q)
    gskip = per_head(jnp.sum(skip_buf[...], axis=0, keepdims=True))

    mine_buf[0] = jnp.concatenate(
        [row(gbias), row(gskip), row(grate), jnp.zeros((5, LANES), F32)], axis=0
    )

    def over_seq(k):
        peer = lax.rem(me + k, nseq)
        return pltpu.make_async_remote_copy(
            src_ref=mine_buf.at[0],
            dst_ref=p1_buf.at[me],
            send_sem=s3.at[k],
            recv_sem=r3.at[k],
            device_id={"seq": peer},
            device_id_type=MESH,
        )

    def over_batch(k):
        peer = lax.rem(my_batch + k, nbatch)
        return pltpu.make_async_remote_copy(
            src_ref=mine_buf.at[1],
            dst_ref=p2_buf.at[my_batch],
            send_sem=s4.at[k],
            recv_sem=r4.at[k],
            device_id={"batch": peer},
            device_id_type=MESH,
        )

    for k in range(1, nseq):
        over_seq(k).start()
    p1_buf[me] = mine_buf[0]
    for k in range(1, nseq):
        over_seq(k).wait()
    total = p1_buf[0]
    for i in range(1, nseq):
        total = total + p1_buf[i]
    mine_buf[1] = total
    for k in range(1, nbatch):
        over_batch(k).start()
    p2_buf[my_batch] = total
    for k in range(1, nbatch):
        over_batch(k).wait()
    total = p2_buf[0]
    for i in range(1, nbatch):
        total = total + p2_buf[i]
    gpar_ref[...] = total * scale
    for b in range(blocks):
        for q in range(parts):
            dx_out(q, b).wait()


def shards(inputs, input_map, output_map, step_raw, step_bias, decay_rate, skip_gain, cotangent):
    tokens, width = inputs.shape[1:]
    heads = step_raw.shape[1]
    states = input_map.shape[2]
    nseq = lax.axis_size("seq")
    nbatch = lax.axis_size("batch")
    blocks = tokens // GROUP
    pw = width // PARTS
    rn = states // nseq
    par = jnp.pad(jnp.stack([step_bias, decay_rate, skip_gain]), ((0, 5), (0, LANES - heads)))
    vmem = pl.BlockSpec(memory_space=pltpu.VMEM)
    hbm = pl.BlockSpec(memory_space=pl.ANY)
    dma = pltpu.SemaphoreType.DMA
    dx, db, dc, draw, gpar = pl.pallas_call(
        functools.partial(kernel, nseq, nbatch, PARTS, 1.0 / math.sqrt(tokens * nseq * nbatch)),
        out_shape=(
            jax.ShapeDtypeStruct((tokens, width), BF),
            jax.ShapeDtypeStruct((tokens, states), F32),
            jax.ShapeDtypeStruct((tokens, states), F32),
            jax.ShapeDtypeStruct((heads, tokens), F32),
            jax.ShapeDtypeStruct((8, LANES), F32),
        ),
        in_specs=[hbm, hbm, vmem, vmem, vmem, vmem],
        out_specs=(hbm, vmem, vmem, vmem, vmem),
        scratch_shapes=[
            pltpu.VMEM((tokens, width), BF),
            pltpu.VMEM((tokens, width), BF),
            pltpu.VMEM((tokens, width), BF),
            pltpu.VMEM((tokens, width), F32),
            pltpu.VMEM((tokens, width), F32),
            pltpu.VMEM((blocks, states, width), F32),
            pltpu.VMEM((blocks, states, width), F32),
            pltpu.VMEM((blocks, 1, width), F32),
            pltpu.VMEM((blocks, heads, GROUP), F32),
            pltpu.VMEM((blocks, GROUP, LANES), BF),
            pltpu.VMEM((blocks, states, GROUP), BF),
            pltpu.VMEM((blocks, states, GROUP), BF),
            pltpu.VMEM((blocks, GROUP, GROUP), BF),
            pltpu.VMEM((blocks, GROUP, GROUP), BF),
            pltpu.VMEM((blocks, GROUP, GROUP), F32),
            pltpu.VMEM((GROUP, 2 * pw), BF),
            pltpu.VMEM((tokens, LANES), F32),
            pltpu.VMEM((PARTS, nseq, 2 * rn, pw), F32),
            pltpu.VMEM((PARTS, nseq, 2 * rn, pw), F32),
            pltpu.VMEM((PARTS, nseq, 2 * rn, pw), F32),
            pltpu.VMEM((PARTS, nseq, 2 * rn, pw), F32),
            pltpu.VMEM((blocks, states, width), BF),
            pltpu.VMEM((blocks, states, width), BF),
            pltpu.VMEM((blocks, 8, width), F32),
            pltpu.VMEM((LANES, width), BF),
            pltpu.VMEM((LANES, width), BF),
            pltpu.VMEM((PARTS, 2 * pw, LANES), BF),
            pltpu.VMEM((8, width), F32),
            pltpu.VMEM((1, width), F32),
            pltpu.VMEM((8, LANES), F32),
            pltpu.VMEM((nseq, 8, LANES), F32),
            pltpu.VMEM((nseq, width), F32),
            pltpu.VMEM((nseq, 8, LANES), F32),
            pltpu.VMEM((nbatch, 8, LANES), F32),
            pltpu.VMEM((2, 8, LANES), F32),
            dma((2, blocks)),
            dma((PARTS, blocks)),
            dma((nseq,)),
            dma((nseq,)),
            dma((PARTS, nseq)),
            dma((PARTS, nseq)),
            dma((PARTS, nseq)),
            dma((PARTS, nseq)),
            dma((nseq,)),
            dma((nseq,)),
            dma((nbatch,)),
            dma((nbatch,)),
        ],
        compiler_params=pltpu.CompilerParams(
            collective_id=0, has_side_effects=True, vmem_limit_bytes=62 << 20
        ),
    )(inputs[0], cotangent[0], input_map[0], output_map[0], step_raw[0], par)
    return dx[None], db[None], dc[None], draw[None], gpar[0:2, 0:heads], gpar[2, 0:heads]


def solution(mesh):
    in_specs = (
        P("batch", "seq", None),
        P("batch", "seq", None),
        P("batch", "seq", None),
        P("batch", None, "seq"),
        P(),
        P(),
        P(),
        P("batch", "seq", None),
    )
    out_specs = (
        P("batch", "seq", None),
        P("batch", "seq", None),
        P("batch", "seq", None),
        P("batch", None, "seq"),
        P(),
        P(),
    )
    return jax.shard_map(shards, mesh=mesh, in_specs=in_specs, out_specs=out_specs, check_vma=False)
```

time: 133 us -> 88 us (0.66)
  Pallas kernels: 121 us -> 76.3 us
    pallas_call x1, Pallas kernels: 121 us -> 76.3 us  [shards(): pl.pallas_call(functools.partial(kernel, nseq, nbatch, PARTS, 1.0 / math....]
where the time goes in v3:
time: 88 us; the launch traced here: 87.8 us
  Pallas kernels  76.3 us (87%)
  local copies, waits for them, and re-layouts  9.57 us (11%)
  other arithmetic  1.29 us (1%)
    pallas_call x1, Pallas kernels, shards(): pl.pallas_call(functools.partial(kernel, nseq, nbatch, PARTS, 1.0 / math....  76.3 us
    unnamed x10, local copies, waits for them, and re-layouts  7.14 us

profile of v3, /device:TPU:1, one launch (start us, length us, event | category | flops | bytes accessed | tf_op | source)
XLA Modules:
  0.0 87.8 jit_solution(15187181421395725972)
XLA Ops:
  0.6 1.3 %select_maximum_fusion.par_ref = f32[8,128]{1,0:T(8,128)} fusion(f32[1,32]{1,0:T(1,128)} %bitcast.23, f32[1,32]{1,0:T(1,128)} %bitcast.24, f32[1,32]{1,0:T(1,128)} %bitcast.25), kind=kLoop, calls=%fused_computation | loop fusion | flops 11264 | bytes 4480 | tf_op jit(solution)/shard_map/stack | solution.py:496
  1.9 76.3 %shard_map.127 = (bf16[1024,2048]{1,0:T(8,128)(2,1)}, f32[1024,128]{1,0:T(8,128)}, f32[1024,128]{1,0:T(8,128)}, f32[32,1024]{1,0:T(8,128)}, f32[8,128]{1,0:T(8,128)}) custom-call(bf16[1024,2048]{1,0:T(8,128)(2,1)} %bitcast.14, bf16[1024,2048]{1,0:T(8,128)(2,1)} %bitcast.15, bf16[1024,128]{1,0:T(8,128)(2,1)} %bitcast.19, bf16[1024,128]{1,0:T(8,128)(2,1)} %bitcast.20, ...), custom_call_target="tpu_custom_call" | custom-call | tf_op jit(solution)/shard_map/pallas_call | solution.py:500
  78.3 1.2 %slice.6 = f32[2,32]{1,0:T(2,128)} slice(f32[8,128]{1,0:T(8,128)} %get-tuple-element.15), slice={[0:2], [0:32]} | slice | bytes 512 | tf_op jit(solution)/shard_map/slice | solution.py:564
  79.5 1.2 %slice_bitcast_fusion = f32[32]{0:T(128)} fusion(f32[8,128]{1,0:T(8,128)} %get-tuple-element.15), kind=kLoop, calls=%fused_computation.4 | loop fusion | bytes 256 | tf_op jit(solution)/shard_map/squeeze | solution.py:564
  80.7 0.0 copy-start.1
  80.7 0.0 copy-start
  80.7 0.0 copy-start.2
  80.7 4.9 %copy.18 = bf16[1,1024,2048]{2,1,0:T(8,128)(2,1)} copy(bf16[1,1024,2048]{2,1,0:T(8,128)(2,1)} %bitcast.16) | data formatting | bytes 8388608
  85.6 0.0 copy-done.1
  85.6 0.8 copy.19
  86.4 0.0 copy-done
  86.4 0.8 copy.20
  87.2 0.0 copy-done.2
  87.2 0.7 copy.21
Async XLA Ops:
  80.7 4.9 %copy-start.1 = (f32[1024,128]{1,0:T(8,128)S(1)}, f32[1024,128]{1,0:T(8,128)}, u32[]{:S(2)}) copy-start(f32[1024,128]{1,0:T(8,128)} %get-tuple-element.12) | copy-start | bytes 1572868
  80.7 5.7 %copy-start = (f32[1024,128]{1,0:T(8,128)S(1)}, f32[1024,128]{1,0:T(8,128)}, u32[]{:S(2)}) copy-start(f32[1024,128]{1,0:T(8,128)} %get-tuple-element.13) | copy-start | bytes 1572868
  80.7 6.5 %copy-start.2 = (f32[32,1024]{1,0:T(8,128)S(1)}, f32[32,1024]{1,0:T(8,128)}, u32[]{:S(2)}) copy-start(f32[32,1024]{1,0:T(8,128)} %get-tuple-element.14) | copy-start | bytes 393220

commit v4 on v3

--- a/solution.py
+++ b/solution.py
@@ -10,7 +10,8 @@
 
 GROUP = 256
 LANES = 128
-PARTS = 4
+UNROLL = True
+PARTS = (256, 512, 512, 512, 256)
 MESH = pl.DeviceIdType.MESH
 BF = jnp.bfloat16
 F32 = jnp.float32
@@ -40,19 +41,22 @@
 def kernel(
     nseq,
     nbatch,
-    parts,
+    cuts,
     scale,
     x_hbm,
     dy_hbm,
     b_ref,
     c_ref,
     raw_ref,
-    par_ref,
+    bias_ref,
+    rate_ref,
+    skip_ref,
     dx_hbm,
     db_ref,
     dc_ref,
     draw_ref,
-    gpar_ref,
+    gpair_ref,
+    grate_ref,
     x_buf,
     dy_buf,
     dyt_buf,
@@ -67,7 +71,6 @@
     ct_buf,
     low_buf,
     up_buf,
-    dsm_buf,
     rc_buf,
     racc_buf,
     send_buf,
@@ -106,9 +109,13 @@
     hs = width // heads
     states = b_ref.shape[1]
     blocks = tokens // GROUP
-    pw = width // parts
-    gw = min(256, pw)
-    groups = pw // gw
+    parts = len(cuts)
+    gw = 256
+    starts = [sum(cuts[:q]) for q in range(parts)]
+
+    def lanes_of(q):
+        return slice(starts[q], starts[q] + cuts[q])
+
     rn = states // nseq
     chunk = max(rn, 16)
     me = lax.axis_index("seq")
@@ -117,15 +124,17 @@
     def rows_of(b):
         return pl.ds(pl.multiple_of(b * GROUP, GROUP), GROUP)
 
-    def x_in(b):
-        return pltpu.make_async_copy(x_hbm.at[rows_of(b)], x_buf.at[rows_of(b)], in_sem.at[0, b])
-
-    def dy_in(b):
-        return pltpu.make_async_copy(dy_hbm.at[rows_of(b)], dy_buf.at[rows_of(b)], in_sem.at[1, b])
-
-    for b in range(blocks):
-        x_in(b).start()
-        dy_in(b).start()
+    def x_in(q):
+        lanes = lanes_of(q)
+        return pltpu.make_async_copy(x_hbm.at[:, lanes], x_buf.at[:, lanes], in_sem.at[0, q])
+
+    def dy_in(q):
+        lanes = lanes_of(q)
+        return pltpu.make_async_copy(dy_hbm.at[:, lanes], dy_buf.at[:, lanes], in_sem.at[1, q])
+
+    for q in range(parts):
+        x_in(q).start()
+        dy_in(q).start()
 
     bar = pltpu.get_barrier_semaphore()
     for k in range(1, nseq):
@@ -142,12 +151,6 @@
     same = (k_id % heads) == l_id
     ohp_buf[...] = jnp.where(same & (k_id < 2 * heads), 1.0, 0.0).astype(BF)
     ohm_buf[...] = jnp.where(same & (k_id >= 2 * heads), 1.0, 0.0).astype(BF)
-    j_id = lax.broadcasted_iota(jnp.int32, (pw, LANES), 1)
-    h_id = lax.broadcasted_iota(jnp.int32, (pw, LANES), 0) // hs
-    for q in range(parts):
-        h_q = h_id + q * (pw // hs)
-        ot_buf[q, 0:pw] = jnp.where(j_id == h_q, 1.0, 0.0).astype(BF)
-        ot_buf[q, pw:] = jnp.where(j_id == h_q + heads, 1.0, 0.0).astype(BF)
 
     eye = lax.broadcasted_iota(jnp.int32, (heads, LANES), 0) == lax.broadcasted_iota(
         jnp.int32, (heads, LANES), 1
@@ -158,7 +161,7 @@
     )
 
     def column(row):
-        return jnp.sum(jnp.where(eye, row, 0.0), axis=1, keepdims=True)
+        return jnp.sum(jnp.where(eye[:, :heads], row, 0.0), axis=1, keepdims=True)
 
     def row(col):
         return jnp.sum(jnp.where(eye, col, 0.0), axis=0, keepdims=True)
@@ -169,9 +172,9 @@
     def per_head(line):
         return jnp.sum(jnp.where(head_lane, line, 0.0), axis=1, keepdims=True)
 
-    bias = column(par_ref[0:1])
-    rate = column(par_ref[1:2])
-    skiprow_buf[...] = expand(column(par_ref[2:3]))
+    bias = column(bias_ref[...])
+    rate = column(rate_ref[...])
+    skiprow_buf[...] = expand(column(skip_ref[...]))
 
     t_id = lax.broadcasted_iota(jnp.int32, (GROUP, GROUP), 0)
     s_id = lax.broadcasted_iota(jnp.int32, (GROUP, GROUP), 1)
@@ -181,37 +184,46 @@
     ones_ge = jnp.where(lower, 1.0, 0.0).astype(BF)
 
     skip_buf[...] = jnp.zeros_like(skip_buf)
-    home_buf[...] = jnp.zeros_like(home_buf)
-
-    def factors(b, total):
-        v = raw_ref[:, rows_of(b)] + bias
-        step = jnp.maximum(v, 0.0) + jnp.log1p(jnp.exp(-jnp.abs(v)))
-        step_buf[b] = step
-        cum = sum_dot(-rate * step, ones_le)
-        ep = jnp.exp(cum)
-        em = step * jnp.exp(-cum)
-        ep_hi, ep_lo = two_parts(ep)
-        em_hi, em_lo = two_parts(em)
-        fac_buf[b] = jnp.concatenate([ep_hi, ep_lo, em_hi, em_lo], axis=0).T.astype(BF)
-        ecl_buf[b] = expand(ep[:, GROUP - 1 : GROUP])
+
+    v_all = raw_ref[...] + bias
+    step_all = jnp.maximum(v_all, 0.0) + jnp.log1p(jnp.exp(-jnp.abs(v_all)))
+    log_all = -rate * step_all
+    step_all = jnp.concatenate(
+        [step_all[:, b * GROUP : (b + 1) * GROUP] for b in range(blocks)], axis=0
+    )
+    log_all = jnp.concatenate(
+        [log_all[:, b * GROUP : (b + 1) * GROUP] for b in range(blocks)], axis=0
+    )
+    cum = sum_dot(log_all, ones_le)
+    ep_all = jnp.exp(cum)
+    em_all = step_all * jnp.exp(-cum)
+    ep_hi, ep_lo = two_parts(ep_all)
+    em_hi, em_lo = two_parts(em_all)
+    total = jnp.ones((heads, 1), F32)
+    for b in range(blocks):
+        hb = slice(b * heads, (b + 1) * heads)
+        step_buf[b] = step_all[hb]
+        fac_buf[b] = jnp.concatenate(
+            [ep_hi[hb], ep_lo[hb], em_hi[hb], em_lo[hb]], axis=0
+        ).T.astype(BF)
+        last = ep_all[hb, GROUP - 1 : GROUP]
+        ecl_buf[b] = expand(last)
+        total = total * last
         bt_buf[b] = b_ref[rows_of(b)].astype(F32).T.astype(BF)
         ct_buf[b] = c_ref[rows_of(b)].astype(F32).T.astype(BF)
-        return total * ep[:, GROUP - 1 : GROUP]
-
-    total = lax.fori_loop(0, blocks, factors, jnp.ones((heads, 1), F32))
     dec_buf[...] = jnp.broadcast_to(row(total), (8, LANES))
 
     def local(q):
+        x_in(q).wait()
+        dy_in(q).wait()
+
         def one_block(b, carry):
             rows = rows_of(b)
-            if q == 0:
-                x_in(b).wait()
-                dy_in(b).wait()
             fac = fac_buf[b]
             bt = bt_buf[b]
             ct = ct_buf[b]
-            for g in range(groups):
-                lanes = slice(q * pw + g * gw, q * pw + (g + 1) * gw)
+            for g in range(cuts[q] // gw):
+                lanes = slice(starts[q] + g * gw, starts[q] + (g + 1) * gw)
                 fp = dot(fac, ohp_buf[:, lanes])
                 fm = dot(fac, ohm_buf[:, lanes])
                 fm_buf[rows, lanes] = fm
@@ -227,8 +239,8 @@
                 dg_buf[b, :, lanes] = dot(ct, dyt)
             return carry
 
-        lax.fori_loop(0, blocks, one_block, 0)
-        lanes = slice(q * pw, (q + 1) * pw)
+        lax.fori_loop(0, blocks, one_block, 0, unroll=UNROLL)
+        lanes = lanes_of(q)
         for j in range(nseq):
             n = slice(j * rn, (j + 1) * rn)
             st = ds_buf[0, n, lanes] * ecl_buf[0, :, lanes]
@@ -239,8 +251,8 @@
                 st = (st + ds_buf[b, n, lanes]) * e
                 gt = gt + decay * dg_buf[b, n, lanes]
                 decay = decay * e
-            send_buf[q, j, 0:rn] = st
-            send_buf[q, j, rn:] = gt
+            send_buf[j, 0:rn, lanes] = st
+            send_buf[j, rn:, lanes] = gt
 
     def decays(k):
         peer = lax.rem(me + k, nseq)
@@ -256,8 +268,8 @@
     def there(q, k):
         peer = lax.rem(me + k, nseq)
         return pltpu.make_async_remote_copy(
-            src_ref=send_buf.at[q, peer],
-            dst_ref=recv_buf.at[q, me],
+            src_ref=send_buf.at[peer, :, lanes_of(q)],
+            dst_ref=recv_buf.at[me, :, lanes_of(q)],
             send_sem=s1.at[q, k],
             recv_sem=r1.at[q, k],
             device_id={"seq": peer},
@@ -267,8 +279,8 @@
     def again(q, k):
         peer = lax.rem(me + k, nseq)
         return pltpu.make_async_remote_copy(
-            src_ref=back_buf.at[q, peer],
-            dst_ref=home_buf.at[q, me],
+            src_ref=back_buf.at[peer, :, lanes_of(q)],
+            dst_ref=home_buf.at[me, :, lanes_of(q)],
             send_sem=s2.at[q, k],
             recv_sem=r2.at[q, k],
             device_id={"seq": peer},
@@ -287,65 +299,65 @@
             rows = rows_of(b)
             low = low_buf[b]
             up = up_buf[b]
-            for g in range(groups):
-                lanes = slice(q * pw + g * gw, q * pw + (g + 1) * gw)
+            for g in range(cuts[q] // gw):
+                lanes = slice(starts[q] + g * gw, starts[q] + (g + 1) * gw)
                 xt = x_buf[rows, lanes]
                 dyt = dyt_buf[rows, lanes]
                 yi = dot(low, xt)
                 dxi = dot(up, dyt)
                 rc_buf[:, g * gw : (g + 1) * gw] = (yi * dyt.astype(F32)).astype(BF)
-                rc_buf[:, pw + g * gw : pw + (g + 1) * gw] = (dxi * xt.astype(F32)).astype(BF)
+                rc_buf[:, cuts[q] + g * gw : cuts[q] + (g + 1) * gw] = (dxi * xt.astype(F32)).astype(BF)
                 dxp_buf[rows, lanes] = fm_buf[rows, lanes] * dxi + skiprow_buf[
                     :, lanes
                 ] * dy_buf[rows, lanes].astype(F32)
-            red = dot(rc_buf[...], ot_buf[q])
-            lanes = slice(q * pw, (q + 1) * pw)
-            ds = dot_nt(dyt_buf[rows, lanes], x_buf[rows, lanes])
+            red = dot(rc_buf[:, 0 : 2 * cuts[q]], ot_buf[2 * starts[q] : 2 * (starts[q] + cuts[q])])
             if q > 0:
                 red = red + racc_buf[rows]
-                ds = ds + dsm_buf[b]
             racc_buf[rows] = red
-            if q < parts - 1:
-                dsm_buf[b] = ds
-            else:
-                ds = jnp.where(lower, ds, 0.0)
-                dc_ref[rows] = dot(ds.astype(BF), b_ref[rows])
-                db_ref[rows] = dot(ds.T.astype(BF), c_ref[rows])
             return carry
 
-        lax.fori_loop(0, blocks, one_block, 0)
+        lax.fori_loop(0, blocks, one_block, 0, unroll=UNROLL)
+
+    def score_grads(b, carry):
+        rows = rows_of(b)
+        ds = jnp.where(lower, dot_nt(dyt_buf[rows], x_buf[rows]), 0.0)
+        dc_ref[rows] = dot(ds.astype(BF), b_ref[rows])
+        db_ref[rows] = dot(ds.T.astype(BF), c_ref[rows])
+        return carry
 
     def scan(q):
-        lanes = slice(q * pw, (q + 1) * pw)
+        lanes = lanes_of(q)
+        pw = cuts[q]
         for k in range(1, nseq):
             there(q, k).wait()
         st = jnp.zeros((rn, pw), F32)
         gt = jnp.zeros((rn, pw), F32)
         for i in range(nseq):
-            back_buf[q, i, 0:rn] = st
-            st = st * decx_buf[i : i + 1, lanes] + recv_buf[q, i, 0:rn]
+            back_buf[i, 0:rn, lanes] = st
+            st = st * decx_buf[i : i + 1, lanes] + recv_buf[i, 0:rn, lanes]
             h = nseq - 1 - i
-            back_buf[q, h, rn:] = gt
-            gt = gt * decx_buf[h : h + 1, lanes] + recv_buf[q, h, rn:]
+            back_buf[h, rn:, lanes] = gt
+            gt = gt * decx_buf[h : h + 1, lanes] + recv_buf[h, rn:, lanes]
         for k in range(1, nseq):
             again(q, k).start()
-        home_buf[q, me] = back_buf[q, me]
+        home_buf[me, :, lanes] = back_buf[me, :, lanes]
 
     def entering(q):
-        lanes = slice(q * pw, (q + 1) * pw)
+        lanes = lanes_of(q)
+        pw = cuts[q]
         for k in range(1, nseq):
             again(q, k).wait()
         dots = [jnp.zeros((8, pw), F32) for _ in range(blocks)]
         for i in range(states // chunk):
             n = slice(i * chunk, (i + 1) * chunk)
             js = range(i * chunk // rn, (i + 1) * chunk // rn)
-            st = jnp.concatenate([home_buf[q, j, 0:rn] for j in js], axis=0)
+            st = jnp.concatenate([home_buf[j, 0:rn, lanes] for j in js], axis=0)
             ends = []
             for b in range(blocks):
                 stb_buf[b, n, lanes] = st.astype(BF)
                 st = (st + ds_buf[b, n, lanes]) * ecl_buf[b, :, lanes]
                 ends.append(st)
-            gt = jnp.concatenate([home_buf[q, j, rn:] for j in js], axis=0)
+            gt = jnp.concatenate([home_buf[j, rn:, lanes] for j in js], axis=0)
             for b in reversed(range(blocks)):
                 prod = gt * ends[b]
                 dots[b] = dots[b] + jnp.sum(prod.reshape(chunk // 8, 8, pw), axis=0)
@@ -356,7 +368,7 @@
             bdot_buf[b, :, lanes] = dots[b]
 
     def dx_out(q, b):
-        lanes = slice(q * pw, (q + 1) * pw)
+        lanes = lanes_of(q)
         return pltpu.make_async_copy(
             dy_buf.at[rows_of(b), lanes], dx_hbm.at[rows_of(b), lanes], out_sem.at[q, b]
         )
@@ -366,23 +378,22 @@
             rows = rows_of(b)
             bb = b_ref[rows]
             cc = c_ref[rows]
-            for g in range(groups):
-                lanes = slice(q * pw + g * gw, q * pw + (g + 1) * gw)
+            for g in range(cuts[q] // gw):
+                lanes = slice(starts[q] + g * gw, starts[q] + (g + 1) * gw)
                 yc = dot(cc, stb_buf[b, :, lanes])
                 dxc = dot(bb, gtb_buf[b, :, lanes])
                 rc_buf[:, g * gw : (g + 1) * gw] = (
                     yc * dyt_buf[rows, lanes].astype(F32)
                 ).astype(BF)
-                rc_buf[:, pw + g * gw : pw + (g + 1) * gw] = (
+                rc_buf[:, cuts[q] + g * gw : cuts[q] + (g + 1) * gw] = (
                     dxc * x_buf[rows, lanes].astype(F32)
                 ).astype(BF)
                 dx = fm_buf[rows, lanes] * dxc + dxp_buf[rows, lanes]
                 dy_buf[rows, lanes] = dx.astype(BF)
             dx_out(q, b).start()
-            lanes = slice(q * pw, (q + 1) * pw)
-            red = racc_buf[rows] + dot(rc_buf[...], ot_buf[q])
-            dc_ref[rows] += dot_nt(dyt_buf[rows, lanes], stb_buf[b, :, lanes])
-            db_ref[rows] += dot_nt(x_buf[rows, lanes], gtb_buf[b, :, lanes])
+            red = racc_buf[rows] + dot(
+                rc_buf[:, 0 : 2 * cuts[q]], ot_buf[2 * starts[q] : 2 * (starts[q] + cuts[q])]
+            )
             if q < parts - 1:
                 racc_buf[rows] = red
                 return carry
@@ -401,20 +412,31 @@
             return gbias, grate
 
         zero = jnp.zeros((heads, 1), F32)
-        return lax.fori_loop(0, blocks, one_block, (zero, zero))
+        return lax.fori_loop(0, blocks, one_block, (zero, zero), unroll=UNROLL)
 
     for q in range(parts):
         local(q)
         if q == 0:
             pl.semaphore_wait(bar, nseq + nbatch - 2)
+        for k in range(1, nseq):
+            there(q, k).start()
+        if q == 0:
             for k in range(1, nseq):
                 decays(k).start()
             decs_buf[me] = dec_buf[...]
-        for k in range(1, nseq):
-            there(q, k).start()
-        recv_buf[q, me] = send_buf[q, me]
-
-    lax.fori_loop(0, blocks, scores, 0)
+        recv_buf[me, :, lanes_of(q)] = send_buf[me, :, lanes_of(q)]
+
+    for q in range(parts):
+        lanes = lanes_of(q)
+        j_id = lax.broadcasted_iota(jnp.int32, (cuts[q], LANES), 1)
+        h_id = (lax.broadcasted_iota(jnp.int32, (cuts[q], LANES), 0) + starts[q]) // hs
+        ot_buf[2 * starts[q] : 2 * starts[q] + cuts[q]] = jnp.where(j_id == h_id, 1.0, 0.0).astype(
+            BF
+        )
+        ot_buf[2 * starts[q] + cuts[q] : 2 * (starts[q] + cuts[q])] = jnp.where(
+            j_id == h_id + heads, 1.0, 0.0
+        ).astype(BF)
+    lax.fori_loop(0, blocks, scores, 0, unroll=UNROLL)
     for q in range(parts):
         inside(q)
         if q == 0:
@@ -429,11 +451,12 @@
                 + dot(low.astype(BF), ohp_buf[...])
             )
         scan(q)
+    lax.fori_loop(0, blocks, score_grads, 0)
+    gskip = per_head(jnp.sum(skip_buf[...], axis=0, keepdims=True))
 
     for q in range(parts):
         entering(q)
         gbias, grate = finish(q)
-    gskip = per_head(jnp.sum(skip_buf[...], axis=0, keepdims=True))
 
     mine_buf[0] = jnp.concatenate(
         [row(gbias), row(gskip), row(grate), jnp.zeros((5, LANES), F32)], axis=0
@@ -464,6 +487,13 @@
     for k in range(1, nseq):
         over_seq(k).start()
     p1_buf[me] = mine_buf[0]
+
+    def map_grads(b, carry):
+        rows = rows_of(b)
+        dc_ref[rows] += dot_nt(dyt_buf[rows], stb_buf[b])
+        return carry
+
+    lax.fori_loop(0, blocks, map_grads, 0)
     for k in range(1, nseq):
         over_seq(k).wait()
     total = p1_buf[0]
@@ -473,12 +503,21 @@
     for k in range(1, nbatch):
         over_batch(k).start()
     p2_buf[my_batch] = total
+
+    def other_grads(b, carry):
+        rows = rows_of(b)
+        db_ref[rows] += dot_nt(x_buf[rows], gtb_buf[b])
+        return carry
+
+    lax.fori_loop(0, blocks, other_grads, 0)
     for k in range(1, nbatch):
         over_batch(k).wait()
     total = p2_buf[0]
     for i in range(1, nbatch):
         total = total + p2_buf[i]
-    gpar_ref[...] = total * scale
+    total = total * scale
+    gpair_ref[...] = total[0:2, 0:heads]
+    grate_ref[...] = total[2:3, 0:heads]
     for b in range(blocks):
         for q in range(parts):
             dx_out(q, b).wait()
@@ -491,23 +530,23 @@
     nseq = lax.axis_size("seq")
     nbatch = lax.axis_size("batch")
     blocks = tokens // GROUP
-    pw = width // PARTS
+    parts = len(PARTS)
     rn = states // nseq
-    par = jnp.pad(jnp.stack([step_bias, decay_rate, skip_gain]), ((0, 5), (0, LANES - heads)))
     vmem = pl.BlockSpec(memory_space=pltpu.VMEM)
     hbm = pl.BlockSpec(memory_space=pl.ANY)
     dma = pltpu.SemaphoreType.DMA
-    dx, db, dc, draw, gpar = pl.pallas_call(
+    dx, db, dc, draw, gpair, grate = pl.pallas_call(
         functools.partial(kernel, nseq, nbatch, PARTS, 1.0 / math.sqrt(tokens * nseq * nbatch)),
         out_shape=(
             jax.ShapeDtypeStruct((tokens, width), BF),
             jax.ShapeDtypeStruct((tokens, states), F32),
             jax.ShapeDtypeStruct((tokens, states), F32),
             jax.ShapeDtypeStruct((heads, tokens), F32),
-            jax.ShapeDtypeStruct((8, LANES), F32),
+            jax.ShapeDtypeStruct((2, heads), F32),
+            jax.ShapeDtypeStruct((1, heads), F32),
         ),
-        in_specs=[hbm, hbm, vmem, vmem, vmem, vmem],
-        out_specs=(hbm, vmem, vmem, vmem, vmem),
+        in_specs=[hbm, hbm] + [vmem] * 6,
+        out_specs=(hbm, vmem, vmem, vmem, vmem, vmem),
         scratch_shapes=[
             pltpu.VMEM((tokens, width), BF),
             pltpu.VMEM((tokens, width), BF),
@@ -523,19 +562,18 @@
             pltpu.VMEM((blocks, states, GROUP), BF),
             pltpu.VMEM((blocks, GROUP, GROUP), BF),
             pltpu.VMEM((blocks, GROUP, GROUP), BF),
-            pltpu.VMEM((blocks, GROUP, GROUP), F32),
-            pltpu.VMEM((GROUP, 2 * pw), BF),
+            pltpu.VMEM((GROUP, 2 * max(PARTS)), BF),
             pltpu.VMEM((tokens, LANES), F32),
-            pltpu.VMEM((PARTS, nseq, 2 * rn, pw), F32),
-            pltpu.VMEM((PARTS, nseq, 2 * rn, pw), F32),
-            pltpu.VMEM((PARTS, nseq, 2 * rn, pw), F32),
-            pltpu.VMEM((PARTS, nseq, 2 * rn, pw), F32),
+            pltpu.VMEM((nseq, 2 * rn, width), F32),
+            pltpu.VMEM((nseq, 2 * rn, width), F32),
+            pltpu.VMEM((nseq, 2 * rn, width), F32),
+            pltpu.VMEM((nseq, 2 * rn, width), F32),
             pltpu.VMEM((blocks, states, width), BF),
             pltpu.VMEM((blocks, states, width), BF),
             pltpu.VMEM((blocks, 8, width), F32),
             pltpu.VMEM((LANES, width), BF),
             pltpu.VMEM((LANES, width), BF),
-            pltpu.VMEM((PARTS, 2 * pw, LANES), BF),
+            pltpu.VMEM((2 * width, LANES), BF),
             pltpu.VMEM((8, width), F32),
             pltpu.VMEM((1, width), F32),
             pltpu.VMEM((8, LANES), F32),
@@ -544,14 +582,14 @@
             pltpu.VMEM((nseq, 8, LANES), F32),
             pltpu.VMEM((nbatch, 8, LANES), F32),
             pltpu.VMEM((2, 8, LANES), F32),
-            dma((2, blocks)),
-            dma((PARTS, blocks)),
+            dma((2, parts)),
+            dma((parts, blocks)),
             dma((nseq,)),
             dma((nseq,)),
-            dma((PARTS, nseq)),
-            dma((PARTS, nseq)),
-            dma((PARTS, nseq)),
-            dma((PARTS, nseq)),
+            dma((parts, nseq)),
+            dma((parts, nseq)),
+            dma((parts, nseq)),
+            dma((parts, nseq)),
             dma((nseq,)),
             dma((nseq,)),
             dma((nbatch,)),
@@ -560,8 +598,17 @@
         compiler_params=pltpu.CompilerParams(
             collective_id=0, has_side_effects=True, vmem_limit_bytes=62 << 20
         ),
-    )(inputs[0], cotangent[0], input_map[0], output_map[0], step_raw[0], par)
-    return dx[None], db[None], dc[None], draw[None], gpar[0:2, 0:heads], gpar[2, 0:heads]
+    )(
+        inputs[0],
+        cotangent[0],
+        input_map[0],
+        output_map[0],
+        step_raw[0],
+        step_bias[None],
+        decay_rate[None],
+        skip_gain[None],
+    )
+    return dx[None], db[None], dc[None], draw[None], gpair, grate[0]
 
 
 def solution(mesh):

time: 88 us -> 83.3 us (0.947)
  Pallas kernels: 76.3 us -> 74.3 us
  local copies, waits for them, and re-layouts: 9.57 us -> 8.21 us
  other arithmetic: 1.29 us -> 0 us
    pallas_call x1, Pallas kernels: 76.3 us -> 74.3 us  [shards(): pl.pallas_call(functools.partial(kernel, nseq, nbatch, PARTS, 1.0 / math....]
    another operation x1 -> x0, other arithmetic: 1.29 us -> none  [shards(): jnp.stack([step_bias, decay_rate, skip_gain])]
    slice x1 -> x0, local copies, waits for them, and re-layouts: 1.25 us -> none  [shards(): gpar[0:2, 0:heads]]
    squeeze x1 -> x0, local copies, waits for them, and re-layouts: 1.19 us -> none  [shards(): gpar[2, 0:heads]]
    unnamed x10 -> x16, local copies, waits for them, and re-layouts: 7.14 us -> 8.21 us
where the time goes in v4:
time: 83.3 us; the launch traced here: 83.2 us
  Pallas kernels  74.3 us (89%)
  local copies, waits for them, and re-layouts  8.21 us (10%)
    pallas_call x1, Pallas kernels, shards(): pl.pallas_call(functools.partial(kernel, nseq, nbatch, PARTS, 1.0 / math....  74.3 us
    unnamed x16, local copies, waits for them, and re-layouts  8.21 us

profile of v4, /device:TPU:1, one launch (start us, length us, event | category | flops | bytes accessed | tf_op | source)
XLA Modules:
  0.0 83.2 jit_solution(12289060955528150628)
XLA Ops:
  0.6 74.3 %shard_map.127 = (bf16[1024,2048]{1,0:T(8,128)(2,1)}, f32[1024,128]{1,0:T(8,128)}, f32[1024,128]{1,0:T(8,128)}, f32[32,1024]{1,0:T(8,128)}, f32[2,32]{1,0:T(2,128)}, /*index=5*/f32[1,32]{1,0:T(1,128)}) custom-call(bf16[1024,2048]{1,0:T(8,128)(2,1)} %bitcast.13, bf16[1024,2048]{1,0:T(8,128)(2,1)} %bitcast.14, bf16[1024,128]{1,0:T(8,128)(2,1)} %bitcast.18, ...), custom_call_target="tpu_custom_call" | custom-call | tf_op jit(solution)/shard_map/pallas_call | solution.py:538
  74.9 0.0 copy-start.1
  74.9 0.0 copy-start
  75.0 0.0 copy-start.2
  75.0 0.0 copy-start.3
  75.0 0.0 copy-start.4
  75.0 4.9 %copy.20 = bf16[1,1024,2048]{2,1,0:T(8,128)(2,1)} copy(bf16[1,1024,2048]{2,1,0:T(8,128)(2,1)} %bitcast.15) | data formatting | bytes 8388608
  79.9 0.0 copy-done.1
  79.9 0.8 copy.21
  80.7 0.0 copy-done
  80.7 0.8 copy.22
  81.5 0.0 copy-done.2
  81.5 0.7 copy.23
  82.1 0.0 copy-done.3
  82.1 0.6 copy.24
  82.7 0.0 copy-done.4
  82.7 0.5 copy.25
Async XLA Ops:
  74.9 4.9 %copy-start.1 = (f32[1024,128]{1,0:T(8,128)S(1)}, f32[1024,128]{1,0:T(8,128)}, u32[]{:S(2)}) copy-start(f32[1024,128]{1,0:T(8,128)} %get-tuple-element.13) | copy-start | bytes 1572868
  74.9 5.7 %copy-start = (f32[1024,128]{1,0:T(8,128)S(1)}, f32[1024,128]{1,0:T(8,128)}, u32[]{:S(2)}) copy-start(f32[1024,128]{1,0:T(8,128)} %get-tuple-element.14) | copy-start | bytes 1572868
  75.0 6.5 %copy-start.2 = (f32[32,1024]{1,0:T(8,128)S(1)}, f32[32,1024]{1,0:T(8,128)}, u32[]{:S(2)}) copy-start(f32[32,1024]{1,0:T(8,128)} %get-tuple-element.15) | copy-start | bytes 393220
  75.0 7.1 %copy-start.3 = (f32[2,32]{1,0:T(2,128)S(1)}, f32[2,32]{1,0:T(2,128)}, u32[]{:S(2)}) copy-start(f32[2,32]{1,0:T(2,128)} %get-tuple-element.28) | copy-start | bytes 772
  75.0 7.7 %copy-start.4 = (f32[1,32]{1,0:T(1,128)S(1)}, f32[1,32]{1,0:T(1,128)}, u32[]{:S(2)}) copy-start(f32[1,32]{1,0:T(1,128)} %get-tuple-element.17) | copy-start | bytes 388

commit v5 on v4

--- a/solution.py
+++ b/solution.py
@@ -11,6 +11,7 @@
 GROUP = 256
 LANES = 128
 UNROLL = True
+CHUNKS = (8, 1, 1, 1)
 PARTS = (256, 512, 512, 512, 256)
 MESH = pl.DeviceIdType.MESH
 BF = jnp.bfloat16
@@ -521,6 +522,33 @@
     for b in range(blocks):
         for q in range(parts):
             dx_out(q, b).wait()
+
+
+def deliver(chunks, *refs):
+    count = len(chunks)
+    buffers = refs[2 * count : 3 * count]
+    sems = refs[3 * count]
+    pairs = []
+    for i in range(count):
+        rows = buffers[i].shape[0] // chunks[i]
+        for c in range(chunks[i]):
+            part = pl.ds(c * rows, rows)
+            k = len(pairs)
+            pairs.append(
+                (
+                    pltpu.make_async_copy(refs[i].at[part], buffers[i].at[part], sems.at[0, k]),
+                    pltpu.make_async_copy(
+                        buffers[i].at[part], refs[count + i].at[part], sems.at[1, k]
+                    ),
+                )
+            )
+    for load, _ in pairs:
+        load.start()
+    for load, store in pairs:
+        load.wait()
+        store.start()
+    for _, store in pairs:
+        store.wait()
 
 
 def shards(inputs, input_map, output_map, step_raw, step_bias, decay_rate, skip_gain, cotangent):
@@ -608,6 +636,16 @@
         decay_rate[None],
         skip_gain[None],
     )
+    arrays = (dx, db, dc, draw)
+    chunks = CHUNKS
+    dx, db, dc, draw = pl.pallas_call(
+        functools.partial(deliver, chunks),
+        out_shape=tuple(jax.ShapeDtypeStruct(a.shape, a.dtype) for a in arrays),
+        in_specs=[hbm] * len(arrays),
+        out_specs=(hbm,) * len(arrays),
+        scratch_shapes=[pltpu.VMEM(a.shape, a.dtype) for a in arrays] + [dma((2, sum(chunks)))],
+        compiler_params=pltpu.CompilerParams(vmem_limit_bytes=62 << 20),
+    )(*arrays)
     return dx[None], db[None], dc[None], draw[None], gpair, grate[0]
 
 

time: 83.3 us -> 80.9 us (0.971)
  local copies, waits for them, and re-layouts: 8.21 us -> 1.08 us
  Pallas kernels: 74.3 us -> 79 us
    unnamed x16 -> x6, local copies, waits for them, and re-layouts: 8.21 us -> 1.08 us
    pallas_call x0 -> x1, Pallas kernels: none -> 4.75 us  [shards(): pl.pallas_call(functools.partial(deliver, chunks), out_shape=tuple((jax.S...]
where the time goes in v5:
time: 80.9 us; the launch traced here: 80.8 us
  Pallas kernels  79 us (98%)
  local copies, waits for them, and re-layouts  1.08 us (1%)
    pallas_call x1, Pallas kernels, shards(): pl.pallas_call(functools.partial(kernel, nseq, nbatch, PARTS, 1.0 / math....  74.3 us
    pallas_call x1, Pallas kernels, shards(): pl.pallas_call(functools.partial(deliver, chunks), out_shape=tuple((jax.S...  4.75 us

profile of v5, /device:TPU:1, one launch (start us, length us, event | category | flops | bytes accessed | tf_op | source)
XLA Modules:
  0.0 80.8 jit_solution(8746784688968716871)
XLA Ops:
  0.6 74.3 %shard_map.127 = (bf16[1024,2048]{1,0:T(8,128)(2,1)}, f32[1024,128]{1,0:T(8,128)}, f32[1024,128]{1,0:T(8,128)}, f32[32,1024]{1,0:T(8,128)}, f32[2,32]{1,0:T(2,128)}, /*index=5*/f32[1,32]{1,0:T(1,128)}) custom-call(bf16[1024,2048]{1,0:T(8,128)(2,1)} %bitcast.13, bf16[1024,2048]{1,0:T(8,128)(2,1)} %bitcast.14, bf16[1024,128]{1,0:T(8,128)(2,1)} %bitcast.15, ...), custom_call_target="tpu_custom_call" | custom-call | tf_op jit(solution)/shard_map/pallas_call | solution.py:566
  74.9 0.0 copy-start
  74.9 0.0 copy-start.1
  74.9 4.8 %shard_map.128 = (bf16[1024,2048]{1,0:T(8,128)(2,1)}, f32[1024,128]{1,0:T(8,128)}, f32[1024,128]{1,0:T(8,128)}, f32[32,1024]{1,0:T(8,128)}) custom-call(bf16[1024,2048]{1,0:T(8,128)(2,1)} %get-tuple-element.16.refs_0_, f32[1024,128]{1,0:T(8,128)} %get-tuple-element.17.refs_1_, f32[1024,128]{1,0:T(8,128)} %get-tuple-element.18.refs_2_, ...), custom_call_target="tpu_custom_call" | custom-call | tf_op jit(solution)/shard_map/pallas_call | solution.py:641
  79.7 0.0 copy-done
  79.7 0.6 copy.16
  80.3 0.0 copy-done.1
  80.3 0.5 copy.17
Async XLA Ops:
  74.9 4.8 %copy-start = (f32[2,32]{1,0:T(2,128)S(1)}, f32[2,32]{1,0:T(2,128)}, u32[]{:S(2)}) copy-start(f32[2,32]{1,0:T(2,128)} %get-tuple-element.36) | copy-start | bytes 772
  74.9 5.3 %copy-start.1 = (f32[1,32]{1,0:T(1,128)S(1)}, f32[1,32]{1,0:T(1,128)}, u32[]{:S(2)}) copy-start(f32[1,32]{1,0:T(1,128)} %get-tuple-element.25) | copy-start | bytes 388

commit v6 on v5

--- a/solution.py
+++ b/solution.py
@@ -46,9 +46,9 @@
     scale,
     x_hbm,
     dy_hbm,
-    b_ref,
-    c_ref,
-    raw_ref,
+    b_hbm,
+    c_hbm,
+    raw_hbm,
     bias_ref,
     rate_ref,
     skip_ref,
@@ -92,6 +92,10 @@
     p1_buf,
     p2_buf,
     mine_buf,
+    b_ref,
+    c_ref,
+    raw_ref,
+    map_sem,
     in_sem,
     out_sem,
     s0,
@@ -133,6 +137,12 @@
         lanes = lanes_of(q)
         return pltpu.make_async_copy(dy_hbm.at[:, lanes], dy_buf.at[:, lanes], in_sem.at[1, q])
 
+    raw_in = pltpu.make_async_copy(raw_hbm, raw_ref, map_sem.at[0])
+    b_in = pltpu.make_async_copy(b_hbm, b_ref, map_sem.at[1])
+    c_in = pltpu.make_async_copy(c_hbm, c_ref, map_sem.at[2])
+    raw_in.start()
+    b_in.start()
+    c_in.start()
     for q in range(parts):
         x_in(q).start()
         dy_in(q).start()
@@ -186,6 +196,7 @@
 
     skip_buf[...] = jnp.zeros_like(skip_buf)
 
+    raw_in.wait()
     v_all = raw_ref[...] + bias
     step_all = jnp.maximum(v_all, 0.0) + jnp.log1p(jnp.exp(-jnp.abs(v_all)))
     log_all = -rate * step_all
@@ -200,6 +211,8 @@
     em_all = step_all * jnp.exp(-cum)
     ep_hi, ep_lo = two_parts(ep_all)
     em_hi, em_lo = two_parts(em_all)
+    b_in.wait()
+    c_in.wait()
     total = jnp.ones((heads, 1), F32)
     for b in range(blocks):
         hb = slice(b * heads, (b + 1) * heads)
@@ -573,7 +586,7 @@
             jax.ShapeDtypeStruct((2, heads), F32),
             jax.ShapeDtypeStruct((1, heads), F32),
         ),
-        in_specs=[hbm, hbm] + [vmem] * 6,
+        in_specs=[hbm] * 5 + [vmem] * 3,
         out_specs=(hbm, vmem, vmem, vmem, vmem, vmem),
         scratch_shapes=[
             pltpu.VMEM((tokens, width), BF),
@@ -610,6 +623,10 @@
             pltpu.VMEM((nseq, 8, LANES), F32),
             pltpu.VMEM((nbatch, 8, LANES), F32),
             pltpu.VMEM((2, 8, LANES), F32),
+            pltpu.VMEM((tokens, states), BF),
+            pltpu.VMEM((tokens, states), BF),
+            pltpu.VMEM((heads, tokens), F32),
+            dma((3,)),
             dma((2, parts)),
             dma((parts, blocks)),
             dma((nseq,)),

time: 80.9 us -> 83.2 us (1.028)
  Pallas kernels: 79 us -> 81.4 us
    pallas_call x1, Pallas kernels: 74.3 us -> 76.6 us  [shards(): pl.pallas_call(functools.partial(kernel, nseq, nbatch, PARTS, 1.0 / math....]
where the time goes in v6:
time: 83.2 us; the launch traced here: 83.1 us
  Pallas kernels  81.4 us (98%)
  local copies, waits for them, and re-layouts  1.08 us (1%)
    pallas_call x1, Pallas kernels, shards(): pl.pallas_call(functools.partial(kernel, nseq, nbatch, PARTS, 1.0 / math....  76.6 us
    pallas_call x1, Pallas kernels, shards(): pl.pallas_call(functools.partial(deliver, chunks), out_shape=tuple((jax.S...  4.75 us

profile of v6, /device:TPU:1, one launch (start us, length us, event | category | flops | bytes accessed | tf_op | source)
XLA Modules:
  0.0 83.1 jit_solution(8437243593366409923)
XLA Ops:
  0.6 76.6 %shard_map.127 = (bf16[1024,2048]{1,0:T(8,128)(2,1)}, f32[1024,128]{1,0:T(8,128)}, f32[1024,128]{1,0:T(8,128)}, f32[32,1024]{1,0:T(8,128)}, f32[2,32]{1,0:T(2,128)}, /*index=5*/f32[1,32]{1,0:T(1,128)}) custom-call(bf16[1024,2048]{1,0:T(8,128)(2,1)} %bitcast.13, bf16[1024,2048]{1,0:T(8,128)(2,1)} %bitcast.14, bf16[1024,128]{1,0:T(8,128)(2,1)} %bitcast.15, ...), custom_call_target="tpu_custom_call" | custom-call | tf_op jit(solution)/shard_map/pallas_call | solution.py:579
  77.2 0.0 copy-start
  77.3 0.0 copy-start.1
  77.3 4.8 %shard_map.128 = (bf16[1024,2048]{1,0:T(8,128)(2,1)}, f32[1024,128]{1,0:T(8,128)}, f32[1024,128]{1,0:T(8,128)}, f32[32,1024]{1,0:T(8,128)}) custom-call(bf16[1024,2048]{1,0:T(8,128)(2,1)} %get-tuple-element.16.refs_0_, f32[1024,128]{1,0:T(8,128)} %get-tuple-element.17.refs_1_, f32[1024,128]{1,0:T(8,128)} %get-tuple-element.18.refs_2_, ...), custom_call_target="tpu_custom_call" | custom-call | tf_op jit(solution)/shard_map/pallas_call | solution.py:658
  82.0 0.0 copy-done
  82.0 0.6 copy.16
  82.6 0.0 copy-done.1
  82.6 0.5 copy.17
Async XLA Ops:
  77.2 4.8 %copy-start = (f32[2,32]{1,0:T(2,128)S(1)}, f32[2,32]{1,0:T(2,128)}, u32[]{:S(2)}) copy-start(f32[2,32]{1,0:T(2,128)} %get-tuple-element.36) | copy-start | bytes 772
  77.3 5.3 %copy-start.1 = (f32[1,32]{1,0:T(1,128)S(1)}, f32[1,32]{1,0:T(1,128)}, u32[]{:S(2)}) copy-start(f32[1,32]{1,0:T(1,128)} %get-tuple-element.25) | copy-start | bytes 388
